TPU v7x, 512 devices: a whole 4x4x16 slice. The times are simulated.
512 devices in a mesh: aa: 16 (over x, y_lo, core), ba: 32 (over y_hi, z).
Axes of the slice: x: 4, y: 4 (y_hi: 2, y_lo: 2; y = y_hi * 2 + y_lo), z: 16, core: 2. Of those that a mesh axis runs over, the one named last changes fastest.
Arguments:
- coefficients: float32 [12288, 12288], P('aa', 'ba'), may hold values from -6 to 6
- tile_values: bfloat16 [16, 3, 768, 768], P('aa'), may hold values from -0.125 to 0.125
- tile_cols: int32 [16, 3], P('aa'), may hold values from 0 to 15, as said below
- alpha_energy: float32 [12288], P('aa'), may hold values from -1 to 1
- beta_energy: float32 [12288], P('ba'), may hold values from -1 to 1
Outputs:
- sigma: float32 [12288, 12288], P('aa', 'ba')
Inputs may be any that keep to these rules, and one draw needn't show every extreme that they name: Row r of tile_cols holds r - 1, r and r + 1 taken modulo 16, each once, in some order.
All inputs are finite; a program needn't handle non-finite values.
Results may differ from a plain program's by a relative error of at most 0.0027.
Values may be sent and summed in bfloat16 or wider, within the bound.
No kernel may reach another device: no remote copies, remote signals or barrier semaphores. Data moves between devices by JAX's collectives and lax.ppermute only.
A program may use at most 64 MiB of HBM per device.

v0:
```python
import jax
import jax.numpy as jnp
from jax import lax
from jax.sharding import PartitionSpec as P


def passed_along(value, axis, steps):
    count = lax.axis_size(axis)
    pairs = [(source, (source + steps) % count) for source in range(count)]
    return lax.ppermute(value, axis, pairs)


def pick_tile(tile_values, tile_cols, target):
    chosen = jnp.zeros(tile_values.shape[2:], tile_values.dtype)
    for slot in range(tile_values.shape[1]):
        chosen = jnp.where(tile_cols[0, slot] == target, tile_values[0, slot], chosen)
    return chosen


def triple_product(tile_values, tile_cols, own_block, from_above, from_below):
    own_index = lax.axis_index("aa")
    cycle_size = lax.axis_size("aa")
    own_tile = pick_tile(tile_values, tile_cols, own_index)
    above_tile = pick_tile(tile_values, tile_cols, (own_index + 1) % cycle_size)
    below_tile = pick_tile(tile_values, tile_cols, (own_index + cycle_size - 1) % cycle_size)
    summed = jnp.dot(own_tile, own_block, preferred_element_type=jnp.float32)
    summed = summed + jnp.dot(above_tile, from_above, preferred_element_type=jnp.float32)
    return summed + jnp.dot(below_tile, from_below, preferred_element_type=jnp.float32)


def body(coefficients, tile_values, tile_cols, alpha_energy, beta_energy):
    coeff_low = coefficients.astype(jnp.bfloat16)
    landed = lax.all_to_all(
        lax.all_to_all(coeff_low, "ba", split_axis=0, concat_axis=1, tiled=True),
        "aa",
        split_axis=1,
        concat_axis=0,
        tiled=True,
    )
    flipped = landed.T
    alpha_up = passed_along(coeff_low, "aa", -1)
    alpha_down = passed_along(coeff_low, "aa", 1)
    alpha_term = triple_product(tile_values, tile_cols, coeff_low, alpha_up, alpha_down)
    beta_up = passed_along(flipped, "aa", -1)
    beta_down = passed_along(flipped, "aa", 1)
    beta_flip = triple_product(tile_values, tile_cols, flipped, beta_up, beta_down)
    beta_term = lax.all_to_all(
        lax.all_to_all(beta_flip.T, "aa", split_axis=0, concat_axis=1, tiled=True),
        "ba",
        split_axis=1,
        concat_axis=0,
        tiled=True,
    )
    energy = alpha_energy[:, None] + beta_energy[None, :]
    return alpha_term + beta_term + energy * coefficients


def solution(mesh):
    in_specs = (P("aa", "ba"), P("aa", None, None, None), P("aa", None), P("aa"), P("ba"))
    out_specs = P("aa", "ba")
    return jax.shard_map(body, mesh=mesh, in_specs=in_specs, out_specs=out_specs, check_vma=False)
```

profile of v0, /device:TPU:33, one launch (start us, length us, event | category | flops | bytes accessed | tf_op | source)
XLA Modules:
  0.0 190.9 jit_solution(9125187930159835711)
XLA Ops:
  0.0 1.3 convert_element_type.3
  1.3 0.8 copy-done
  2.2 52.5 %all_to_all.70 = bf16[32,24,384]{2,1,0:T(8,128)(2,1)S(1)} all-to-all(bf16[32,24,384]{2,1,0:T(8,128)(2,1)S(1)} %bitcast.38), channel_id=1, replica_groups=mesh['aa'=16,'ba'=32] {'ba'}, dimensions={0} | all-to-all | bytes 1179648 | tf_op jit(solution)/shard_map/all_to_all | solution.py:34
  54.6 0.1 copy.10
  54.7 0.2 all_to_all.55
  54.9 0.0 copy-start.2
  54.9 1.0 copy.11
  55.9 6.8 %all-to-all-start.1 = ((bf16[24,16,768]{2,0,1:T(8,128)(2,1)}), bf16[24,16,768]{2,0,1:T(8,128)(2,1)}, u32[]{:S(2)}, u32[]{:S(2)}) async-start(bf16[24,16,768]{2,0,1:T(8,128)(2,1)} %copy.11), calls=%async_computation.1 | async-start | bytes 1179648 | tf_op jit(solution)/shard_map/all_to_all | solution.py:33
  62.7 0.6 fusion.10
  69.0 4.0 %all-to-all-done.1 = bf16[24,16,768]{2,0,1:T(8,128)(2,1)} async-done(((bf16[24,16,768]{2,0,1:T(8,128)(2,1)}), bf16[24,16,768]{2,0,1:T(8,128)(2,1)}, u32[]{:S(2)}, u32[]{:S(2)}) %all-to-all-start.1) | async-done | bytes 589856 | tf_op jit(solution)/shard_map/all_to_all | solution.py:33
  73.0 3.3 %collective-permute-start.2 = (bf16[768,384]{0,1:T(8,128)(2,1)}, bf16[768,384]{0,1:T(8,128)(2,1)S(1)}, u32[]{:S(2)}, u32[]{:S(2)}) collective-permute-start(bf16[768,384]{0,1:T(8,128)(2,1)} %bitcast.11), channel_id=1, source_target_pairs={{0,480},{32,0},{64,32},{96,64},{128,96},{160,128},{192,160},{224,1... | collective-permute-start | bytes 1769480 | tf_op jit(solution)/shard_map/ppermute | solution.py:10
  76.3 2.3 %select_select_fusion = (bf16[1,1,768,768]{3,2,1,0:T(8,128)(2,1)S(1)}, bf16[1,1,768,768]{3,2,1,0:T(8,128)(2,1)S(1)}, bf16[1,1,768,768]{3,2,1,0:T(8,128)(2,1)S(1)}) fusion(pred[]{:T(512)S(6)} %eq.49, pred[]{:T(512)S(6)} %eq.48, pred[]{:T(512)S(6)} %eq.47, bf16[1,3,768,768]{3,2,1,0:T(8,128)(2,1)} %param.6, pred[]{:T(512)S(6)} %eq.43, pred[]{:T(512)S(6)} %eq.42, ...), kind=kLoop, calls=%fused_computation.14 | loop fusion | flops 5308416 | bytes 7077897 | tf_op jit(solution)/shard_map/jit(_where)/select_n | solution.py:16
  78.7 2.3 %collective-permute-start.3 = (bf16[768,384]{0,1:T(8,128)(2,1)}, bf16[768,384]{0,1:T(8,128)(2,1)S(1)}, u32[]{:S(2)}, u32[]{:S(2)}) collective-permute-start(bf16[768,384]{0,1:T(8,128)(2,1)} %bitcast.11), channel_id=1, source_target_pairs={{0,32},{32,64},{64,96},{96,128},{128,160},{160,192},{192,224},{224... | collective-permute-start | bytes 1769480 | tf_op jit(solution)/shard_map/ppermute | solution.py:10
  80.9 1.7 fusion.6
  82.6 1.8 collective-permute-done.2
  84.4 0.7 convolution_add_fusion.1
  85.1 6.0 %collective-permute-done.3 = bf16[768,384]{0,1:T(8,128)(2,1)S(1)} collective-permute-done((bf16[768,384]{0,1:T(8,128)(2,1)}, bf16[768,384]{0,1:T(8,128)(2,1)S(1)}, u32[]{:S(2)}, u32[]{:S(2)}) %collective-permute-start.3) | collective-permute-done | bytes 589856 | tf_op jit(solution)/shard_map/ppermute | solution.py:10
  91.1 0.7 convolution_add_fusion
  91.8 22.2 %all_to_all.71 = f32[16,24,768]{2,1,0:T(8,128)S(1)} all-to-all(f32[16,24,768]{2,1,0:T(8,128)S(1)} %bitcast.40), channel_id=1, replica_groups=mesh['aa'=16,'ba'=32] {'aa'}, dimensions={0} | all-to-all | bytes 2359296 | tf_op jit(solution)/shard_map/all_to_all | solution.py:48
  113.9 1.4 copy.12
  115.3 2.5 %all_to_all.62 = f32[24,32,384]{2,1,0:T(8,128)} reshape(f32[24,16,768]{2,1,0:T(8,128)} %copy.12) | data formatting | bytes 2359296 | tf_op jit(solution)/shard_map/all_to_all | solution.py:47
  117.8 3.0 %copy.13 = f32[24,32,384]{2,0,1:T(8,128)} copy(f32[24,32,384]{2,1,0:T(8,128)} %all_to_all.62) | data formatting | bytes 2359296 | tf_op jit(solution)/shard_map/all_to_all | solution.py:47
  120.8 4.4 %all-to-all-start.3 = ((f32[24,32,384]{2,0,1:T(8,128)}), f32[24,32,384]{2,0,1:T(8,128)}, u32[]{:S(2)}, u32[]{:S(2)}) async-start(f32[24,32,384]{2,0,1:T(8,128)} %copy.13), calls=%async_computation.3 | async-start | bytes 2359296 | tf_op jit(solution)/shard_map/all_to_all | solution.py:47
  125.2 2.8 %collective-permute-start = (bf16[768,384]{1,0:T(8,128)(2,1)}, bf16[768,384]{1,0:T(8,128)(2,1)S(1)}, u32[]{:S(2)}, u32[]{:S(2)}) collective-permute-start(bf16[768,384]{1,0:T(8,128)(2,1)} %copy-done), channel_id=1, source_target_pairs={{0,480},{32,0},{64,32},{96,64},{128,96},{160,128},{192,160},{224,1... | collective-permute-start | bytes 1769480 | tf_op jit(solution)/shard_map/ppermute | solution.py:10
  128.0 2.8 %collective-permute-start.1 = (bf16[768,384]{1,0:T(8,128)(2,1)}, bf16[768,384]{1,0:T(8,128)(2,1)}, u32[]{:S(2)}, u32[]{:S(2)}) collective-permute-start(bf16[768,384]{1,0:T(8,128)(2,1)} %copy-done), channel_id=1, source_target_pairs={{0,32},{32,64},{64,96},{96,128},{128,160},{160,192},{192,224},{224... | collective-permute-start | bytes 1769480 | tf_op jit(solution)/shard_map/ppermute | solution.py:10
  130.8 1.8 fusion.8
  132.6 0.0 copy-start.1
  132.6 0.0 copy-start.3
  132.7 13.9 %collective-permute-done = bf16[768,384]{1,0:T(8,128)(2,1)S(1)} collective-permute-done((bf16[768,384]{1,0:T(8,128)(2,1)}, bf16[768,384]{1,0:T(8,128)(2,1)S(1)}, u32[]{:S(2)}, u32[]{:S(2)}) %collective-permute-start) | collective-permute-done | bytes 589856 | tf_op jit(solution)/shard_map/ppermute | solution.py:10
  146.5 1.8 convolution_add_fusion.3
  148.3 39.0 %all-to-all-done.3 = f32[24,32,384]{2,0,1:T(8,128)} async-done(((f32[24,32,384]{2,0,1:T(8,128)}), f32[24,32,384]{2,0,1:T(8,128)}, u32[]{:S(2)}, u32[]{:S(2)}) %all-to-all-start.3) | async-done | bytes 1179680 | tf_op jit(solution)/shard_map/all_to_all | solution.py:47
  187.3 3.6 %fusion.1 = f32[768,384]{1,0:T(8,128)} fusion(f32[768,384]{1,0:T(8,128)} %bitcast.17, f32[768,384]{1,0:T(8,128)} %convolution_add_fusion.3, bf16[768,384]{1,0:T(8,128)(2,1)} %collective-permute-done.1, bf16[1,1,768,768]{3,2,1,0:T(8,128)(2,1)S(1)} %get-tuple-element.5, f32[768,384]{1,0:T(8,128)S(1)} %copy-done.1, f32[384]{0:T(512)S(1)} %copy-done.4, ...), kind=kOutput, calls=%fused_computation.4 | convolution fusion | flops 454459392 | bytes 6492672 | tf_op jit(solution)/shard_map/dot_general | solution.py:28
  (7 shorter events, 0.0 us)
Async XLA Ops:
  1.3 0.8 copy-start
  54.9 7.8 %copy-start.2 = (s32[1,3]{1,0:T(1,128)S(1)}, s32[1,3]{1,0:T(1,128)}, u32[]{:S(2)}) copy-start(s32[1,3]{1,0:T(1,128)} %param.7) | copy-start | bytes 40
  55.9 17.1 %all-to-all-start.1 = ((bf16[24,16,768]{2,0,1:T(8,128)(2,1)}), bf16[24,16,768]{2,0,1:T(8,128)(2,1)}, u32[]{:S(2)}, u32[]{:S(2)}) async-start(bf16[24,16,768]{2,0,1:T(8,128)(2,1)} %copy.11), calls=%async_computation.1 | async-start | bytes 1179648 | tf_op jit(solution)/shard_map/all_to_all | solution.py:33
  73.0 11.4 %collective-permute-start.2 = (bf16[768,384]{0,1:T(8,128)(2,1)}, bf16[768,384]{0,1:T(8,128)(2,1)S(1)}, u32[]{:S(2)}, u32[]{:S(2)}) collective-permute-start(bf16[768,384]{0,1:T(8,128)(2,1)} %bitcast.11), channel_id=1, source_target_pairs={{0,480},{32,0},{64,32},{96,64},{128,96},{160,128},{192,160},{224,1... | collective-permute-start | bytes 1769480 | tf_op jit(solution)/shard_map/ppermute | solution.py:10
  78.7 12.5 %collective-permute-start.3 = (bf16[768,384]{0,1:T(8,128)(2,1)}, bf16[768,384]{0,1:T(8,128)(2,1)S(1)}, u32[]{:S(2)}, u32[]{:S(2)}) collective-permute-start(bf16[768,384]{0,1:T(8,128)(2,1)} %bitcast.11), channel_id=1, source_target_pairs={{0,32},{32,64},{64,96},{96,128},{128,160},{160,192},{192,224},{224... | collective-permute-start | bytes 1769480 | tf_op jit(solution)/shard_map/ppermute | solution.py:10
  120.8 66.6 %all-to-all-start.3 = ((f32[24,32,384]{2,0,1:T(8,128)}), f32[24,32,384]{2,0,1:T(8,128)}, u32[]{:S(2)}, u32[]{:S(2)}) async-start(f32[24,32,384]{2,0,1:T(8,128)} %copy.13), calls=%async_computation.3 | async-start | bytes 2359296 | tf_op jit(solution)/shard_map/all_to_all | solution.py:47
  125.2 21.3 %collective-permute-start = (bf16[768,384]{1,0:T(8,128)(2,1)}, bf16[768,384]{1,0:T(8,128)(2,1)S(1)}, u32[]{:S(2)}, u32[]{:S(2)}) collective-permute-start(bf16[768,384]{1,0:T(8,128)(2,1)} %copy-done), channel_id=1, source_target_pairs={{0,480},{32,0},{64,32},{96,64},{128,96},{160,128},{192,160},{224,1... | collective-permute-start | bytes 1769480 | tf_op jit(solution)/shard_map/ppermute | solution.py:10
  128.0 20.4 %collective-permute-start.1 = (bf16[768,384]{1,0:T(8,128)(2,1)}, bf16[768,384]{1,0:T(8,128)(2,1)}, u32[]{:S(2)}, u32[]{:S(2)}) collective-permute-start(bf16[768,384]{1,0:T(8,128)(2,1)} %copy-done), channel_id=1, source_target_pairs={{0,32},{32,64},{64,96},{96,128},{128,160},{160,192},{192,224},{224... | collective-permute-start | bytes 1769480 | tf_op jit(solution)/shard_map/ppermute | solution.py:10
  132.6 54.7 %copy-start.1 = (f32[768,384]{1,0:T(8,128)S(1)}, f32[768,384]{1,0:T(8,128)}, u32[]{:S(2)}) copy-start(f32[768,384]{1,0:T(8,128)} %param.5) | copy-start | bytes 3538948
  132.6 54.7 %copy-start.3 = (f32[768]{0:T(1024)S(1)}, f32[768]{0:T(1024)}, u32[]{:S(2)}) copy-start(f32[768]{0:T(1024)} %param.8) | copy-start | bytes 9220
  132.7 54.7 %copy-start.4 = (f32[384]{0:T(512)S(1)}, f32[384]{0:T(512)}, u32[]{:S(2)}) copy-start(f32[384]{0:T(512)} %param.9) | copy-start | bytes 4612
where the time goes:
time: 192 us; the launch traced here: 191 us
  blocking collectives  74.6 us (39%)
  waiting for transfers between devices  64.7 us (34%)
  starting transfers between devices  22.3 us (12%)
  matrix products  10.3 us (5%)
  local copies, waits for them, and re-layouts  9.54 us (5%)
  between operations  5.79 us (3%)
  other arithmetic  3.67 us (2%)
    all_to_all x1, blocking collectives, body(): lax.all_to_all(coeff_low, 'ba', split_axis=0, concat_axis=1, tiled=True)  52.5 us
    all_to_all x1, waiting for transfers between devices, body(): lax.all_to_all(lax.all_to_all(beta_flip.T, 'aa', split_axis=0, concat_axi...  39 us
    all_to_all x1, blocking collectives, body(): lax.all_to_all(beta_flip.T, 'aa', split_axis=0, concat_axis=1, tiled=True)  22.2 us
    ppermute x4, waiting for transfers between devices, passed_along(): return lax.ppermute(value, axis, pairs)  21.7 us
    ppermute x4, starting transfers between devices, passed_along(): return lax.ppermute(value, axis, pairs)  11.1 us
    all_to_all x1, starting transfers between devices, body(): lax.all_to_all(lax.all_to_all(coeff_low, 'ba', split_axis=0, concat_axis=...  6.77 us
    all_to_all x2, local copies, waits for them, and re-layouts, body(): lax.all_to_all(lax.all_to_all(beta_flip.T, 'aa', split_axis=0, concat_axi...  5.42 us
    all_to_all x1, starting transfers between devices, body(): lax.all_to_all(lax.all_to_all(beta_flip.T, 'aa', split_axis=0, concat_axi...  4.45 us
  transfers between devices with their start and end apart: 6, of which 5 were waited for; matrix products, arithmetic and copies ran while one was open for 5% of the time, Pallas kernels for 0%

commit v1 on v0

v1 whole, which is shorter than its diff:
```python
import jax
import jax.numpy as jnp
from jax import lax
from jax.experimental import pallas as pl
from jax.experimental.pallas import tpu as pltpu
from jax.sharding import PartitionSpec as P


BOTH = ("aa", "ba")
ANY = pl.BlockSpec(memory_space=pl.ANY)
SCALARS = pl.BlockSpec(memory_space=pltpu.SMEM)
SMALL = pltpu.CompilerParams(vmem_limit_bytes=4 * 1024 * 1024)


def pick(tile_cols, tile_values):
    rows = lax.axis_size("aa")
    tile = tile_values.shape[2]
    chunk, quarter = tile // 2, tile // 4

    def kernel(cols_ref, tiles_ref, own_ref, other_ref, sems):
        row = lax.axis_index("aa")
        half = lax.rem(lax.axis_index("ba"), 2)
        core = lax.rem(row, 2)

        def copy(out_ref, core_of, t):
            place = jnp.where(half == 1, 5 - t, t)
            block = lax.rem(row + lax.div(place, 2) + rows - 1, rows)
            slot = jnp.where(cols_ref[0, 1] == block, 1, jnp.where(cols_ref[0, 2] == block, 2, 0))
            start = pl.multiple_of(half * chunk + core_of * quarter, 64)
            side = pl.multiple_of(lax.rem(place, 2) * chunk, 128)
            source = tiles_ref.at[0, slot, pl.ds(start, quarter), pl.ds(side, chunk)]
            return pltpu.make_async_copy(source, out_ref.at[t], sems.at[t + (6 if out_ref is other_ref else 0)])

        copies = [copy(other_ref, 1 - core, t) for t in range(6)] + [copy(own_ref, core, t) for t in range(6)]
        for each in copies:
            each.start()
        for each in copies:
            each.wait()

    shape = jax.ShapeDtypeStruct((6, quarter, chunk), jnp.bfloat16)
    return pl.pallas_call(
        kernel,
        out_shape=(shape, shape),
        in_specs=[SCALARS, ANY],
        out_specs=(ANY, ANY),
        scratch_shapes=[pltpu.SemaphoreType.DMA((12,))],
        compiler_params=SMALL,
        name="pick",
    )(tile_cols, tile_values)


def arrange(mine, theirs):
    count, parts, piece, chunk = mine.shape

    def kernel(mine_ref, theirs_ref, out_ref, sems):
        place = lax.axis_index("aa")
        x, core = lax.div(place, 4), lax.rem(place, 2)
        copies = []
        for index, (source, core_of) in enumerate(((mine_ref, core), (theirs_ref, 1 - core))):
            for step in range(count):
                at = pl.multiple_of(core_of * count * piece + lax.rem(x + step, count) * piece, 16)
                target = out_ref.at[:, pl.ds(at, piece), :]
                copies.append(pltpu.make_async_copy(source.at[step], target, sems.at[index * count + step]))
        for each in copies:
            each.start()
        for each in copies:
            each.wait()

    return pl.pallas_call(
        kernel,
        out_shape=jax.ShapeDtypeStruct((parts, 2 * count * piece, chunk), jnp.bfloat16),
        in_specs=[ANY, ANY],
        out_specs=ANY,
        scratch_shapes=[pltpu.SemaphoreType.DMA((2 * count,))],
        compiler_params=SMALL,
        name="arrange",
    )(mine, theirs)


def times(left, right):
    return lax.dot_general(left, right, (((1,), (1,)), ((), ())), preferred_element_type=jnp.float32)


def spread_pairs(step, cols):
    pairs = []
    for b in range(cols):
        row, upper, depth = b // 2, b // 16, b % 16
        for core in range(2):
            for y in range(2):
                x_of, y_of = row // 4, (row // 2) % 2
                source_upper = upper if y == y_of else 1 - upper
                source = (x_of * 4 + y_of * 2 + core) * cols + source_upper * 16 + depth
                target = (((x_of + step) % 4) * 4 + y * 2 + core) * cols + b
                pairs.append((source, target))
    return pairs


def body(coefficients, tile_values, tile_cols, alpha_energy, beta_energy):
    rows, cols = lax.axis_size("aa"), lax.axis_size("ba")
    tile, chunk = coefficients.shape
    a, depth = lax.axis_index("aa"), lax.axis_index("ba") % 16
    across = [(j, (j + 1) % cols if j % 2 else (j - 1) % cols) for j in range(cols)]
    within = [(j, j ^ 1) for j in range(cols)]

    low = coefficients.astype(jnp.bfloat16)
    near = lax.ppermute(low, "ba", across)
    sibling = lax.ppermute(low, "ba", within)

    own_half, other_half = pick(tile_cols, tile_values)
    holders = [
        (i * cols + j, (i ^ 1) * cols + j) for i in range(rows) for j in range(cols) if i % 8 == (j % 16) // 2
    ]
    passed = lax.ppermute(other_half, BOTH, holders)
    held = jnp.where(a % 8 == depth // 2, own_half, passed).reshape(6, 4, tile // 16, chunk)
    got = 0
    for step in (2, 1, 3, 0):
        part = lax.dynamic_index_in_dim(held, ((a // 4) + step) % 4, 1, keepdims=False)
        got = got + lax.ppermute(part, BOTH, spread_pairs(step, cols))

    above = lax.ppermute(low, "aa", [(i, (i - 1) % rows) for i in range(rows)])
    below = lax.ppermute(low, "aa", [(i, (i + 1) % rows) for i in range(rows)])
    far = lax.ppermute(sibling, "ba", across)
    next_near = lax.ppermute(near, "ba", within)
    next_far = lax.ppermute(far, "ba", within)

    pieces = {0: got}
    for step in (2, 1, 3):
        pieces[step] = lax.ppermute(got, "aa", [(i, (i - 4 * step) % rows) for i in range(rows)])
    mine = jnp.stack([pieces[step] for step in range(4)])
    theirs = lax.ppermute(mine, "aa", [(i, i ^ 1) for i in range(rows)])
    weight = arrange(mine, theirs)

    slots = jnp.arange(3, dtype=jnp.int32)

    def tile_of(block):
        slot = jnp.sum(jnp.where(tile_cols[0] == block, slots, 0))
        return lax.dynamic_slice(tile_values, (0, slot, 0, 0), (1, 1, tile, tile))[0, 0]

    total = jnp.dot(tile_of(a), low, preferred_element_type=jnp.float32)
    total = total + jnp.dot(tile_of((a + 1) % rows), above, preferred_element_type=jnp.float32)
    total = total + jnp.dot(tile_of((a + rows - 1) % rows), below, preferred_element_type=jnp.float32)
    total = total + (alpha_energy[:, None] + beta_energy[None, :]) * coefficients
    for index, value in enumerate((far, near, low, sibling, next_near, next_far)):
        total = total + times(value, weight[index])
    return total


def solution(mesh):
    in_specs = (P("aa", "ba"), P("aa", None, None, None), P("aa", None), P("aa"), P("ba"))
    out_specs = P("aa", "ba")
    return jax.shard_map(body, mesh=mesh, in_specs=in_specs, out_specs=out_specs, check_vma=False)
```

time: 192 us -> 108 us (0.56)
  the two profiles are of different devices: /device:TPU:33 before, /device:TPU:8 now
where the time goes in v1:
time: 108 us; the launch traced here: 107 us
  starting transfers between devices  44.9 us (42%)
  waiting for transfers between devices  36 us (33%)
  matrix products  11.9 us (11%)
  between operations  6.13 us (6%)
  other arithmetic  3.85 us (4%)
  local copies, waits for them, and re-layouts  2.81 us (3%)
  Pallas kernels  1.45 us (1%)
    ppermute x1, waiting for transfers between devices, body(): far = lax.ppermute(sibling, 'ba', across)  14.3 us
    ppermute x1, starting transfers between devices, body(): near = lax.ppermute(low, 'ba', across)  14.2 us
    ppermute x4, waiting for transfers between devices, body(): got = got + lax.ppermute(part, BOTH, spread_pairs(step, cols))  12.9 us
    ppermute x3, starting transfers between devices, body(): lax.ppermute(got, 'aa', [(i, (i - 4 * step) % rows) for i in range(rows)])  10.2 us
    ppermute x1, waiting for transfers between devices, body(): next_far = lax.ppermute(far, 'ba', within)  8.41 us
    dot_general x6, matrix products, times(): lax.dot_general(left, right, (((1,), (1,)), ((), ())), preferred_element_...  7.4 us
    ppermute x1, starting transfers between devices, body(): sibling = lax.ppermute(low, 'ba', within)  3.95 us
    ppermute x4, starting transfers between devices, body(): got = got + lax.ppermute(part, BOTH, spread_pairs(step, cols))  3.45 us
  transfers between devices with their start and end apart: 16, of which 4 were waited for; matrix products, arithmetic and copies ran while one was open for 12% of the time, Pallas kernels for 0%

profile of v1, /device:TPU:8, one launch (start us, length us, event | category | flops | bytes accessed | tf_op | source)
XLA Modules:
  0.0 107.0 jit_solution(17171953549383827144)
XLA Ops:
  0.0 2.0 %copy-done = bf16[1,3,768,768]{3,2,1,0:T(8,128)(2,1)S(1)} copy-done((bf16[1,3,768,768]{3,2,1,0:T(8,128)(2,1)S(1)}, bf16[1,3,768,768]{3,2,1,0:T(8,128)(2,1)}, u32[]{:S(2)}) %copy-start) | copy-done | bytes 3538968
  2.7 0.9 pick.1
  3.6 0.7 collective-permute-start.2
  4.7 0.8 collective-permute-start.3
  5.5 0.7 collective-permute-start.4
  6.2 0.7 collective-permute-start.5
  6.9 1.3 %collective-permute-start.6 = (bf16[6,48,384]{2,1,0:T(8,128)(2,1)S(1)}, bf16[6,48,384]{2,1,0:T(8,128)(2,1)S(1)}, u32[]{:S(2)}, u32[]{:S(2)}) collective-permute-start(bf16[6,48,384]{2,1,0:T(8,128)(2,1)S(1)} %get-tuple-element.15), channel_id=1, source_target_pairs={{0,0},{16,64},{32,32},{48,96},{1,1},{17,65},{33,33},{49,97},{2,2},... | collective-permute-start | bytes 663560 | tf_op jit(solution)/shard_map/ppermute | solution.py:118
  8.2 12.9 %collective-permute-done.6 = bf16[6,48,384]{2,1,0:T(8,128)(2,1)S(1)} collective-permute-done((bf16[6,48,384]{2,1,0:T(8,128)(2,1)S(1)}, bf16[6,48,384]{2,1,0:T(8,128)(2,1)S(1)}, u32[]{:S(2)}, u32[]{:S(2)}) %collective-permute-start.6) | collective-permute-done | bytes 221216 | tf_op jit(solution)/shard_map/ppermute | solution.py:118
  21.1 0.8 add_add_fusion
  21.9 3.4 %collective-permute-start.7 = (bf16[6,48,384]{2,1,0:T(8,128)(2,1)}, bf16[6,48,384]{2,1,0:T(8,128)(2,1)}, u32[]{:S(2)}, u32[]{:S(2)}) collective-permute-start(bf16[6,48,384]{2,1,0:T(8,128)(2,1)} %add_add_fusion), channel_id=1, source_target_pairs={{0,384},{32,416},{64,448},{96,480},{128,0},{160,32},{192,64},{224,... | collective-permute-start | bytes 663560 | tf_op jit(solution)/shard_map/ppermute | solution.py:128
  25.3 4.9 %collective-permute-start.8 = (bf16[6,48,384]{2,1,0:T(8,128)(2,1)}, bf16[6,48,384]{2,1,0:T(8,128)(2,1)}, u32[]{:S(2)}, u32[]{:S(2)}) collective-permute-start(bf16[6,48,384]{2,1,0:T(8,128)(2,1)} %add_add_fusion), channel_id=1, source_target_pairs={{0,256},{32,288},{64,320},{96,352},{128,384},{160,416},{192,448},{... | collective-permute-start | bytes 663560 | tf_op jit(solution)/shard_map/ppermute | solution.py:128
  30.2 1.9 %collective-permute-start.9 = (bf16[6,48,384]{2,1,0:T(8,128)(2,1)}, bf16[6,48,384]{2,1,0:T(8,128)(2,1)}, u32[]{:S(2)}, u32[]{:S(2)}) collective-permute-start(bf16[6,48,384]{2,1,0:T(8,128)(2,1)} %add_add_fusion), channel_id=1, source_target_pairs={{0,128},{32,160},{64,192},{96,224},{128,256},{160,288},{192,320},{... | collective-permute-start | bytes 663560 | tf_op jit(solution)/shard_map/ppermute | solution.py:128
  32.2 0.9 convert_element_type.3
  33.1 3.9 %collective-permute-start.11 = (bf16[768,384]{1,0:T(8,128)(2,1)}, bf16[768,384]{1,0:T(8,128)(2,1)}, u32[]{:S(2)}, u32[]{:S(2)}) collective-permute-start(bf16[768,384]{1,0:T(8,128)(2,1)} %convert_element_type.3), channel_id=1, source_target_pairs={{0,1},{1,0},{2,3},{3,2},{4,5},{5,4},{6,7},{7,6},{8,9},{9,8},{10,11... | collective-permute-start | bytes 1769480 | tf_op jit(solution)/shard_map/ppermute | solution.py:107
  37.0 14.2 %collective-permute-start.13 = (bf16[768,384]{1,0:T(8,128)(2,1)}, bf16[768,384]{1,0:T(8,128)(2,1)}, u32[]{:S(2)}, u32[]{:S(2)}) collective-permute-start(bf16[768,384]{1,0:T(8,128)(2,1)} %convert_element_type.3), channel_id=1, source_target_pairs={{0,31},{1,2},{2,1},{3,4},{4,3},{5,6},{6,5},{7,8},{8,7},{9,10},{10,... | collective-permute-start | bytes 1769480 | tf_op jit(solution)/shard_map/ppermute | solution.py:106
  51.2 1.9 %collective-permute-start = (bf16[768,384]{1,0:T(8,128)(2,1)}, bf16[768,384]{1,0:T(8,128)(2,1)}, u32[]{:S(2)}, u32[]{:S(2)}) collective-permute-start(bf16[768,384]{1,0:T(8,128)(2,1)} %convert_element_type.3), channel_id=1, source_target_pairs={{0,480},{32,0},{64,32},{96,64},{128,96},{160,128},{192,160},{224,1... | collective-permute-start | bytes 1769480 | tf_op jit(solution)/shard_map/ppermute | solution.py:120
  53.1 0.7 fusion.19
  59.4 2.4 %collective-permute-start.1 = (bf16[768,384]{1,0:T(8,128)(2,1)}, bf16[768,384]{1,0:T(8,128)(2,1)S(1)}, u32[]{:S(2)}, u32[]{:S(2)}) collective-permute-start(bf16[768,384]{1,0:T(8,128)(2,1)} %convert_element_type.3), channel_id=1, source_target_pairs={{0,32},{32,64},{64,96},{96,128},{128,160},{160,192},{192,224},{224... | collective-permute-start | bytes 1769480 | tf_op jit(solution)/shard_map/ppermute | solution.py:121
  61.9 1.4 %pad_maximum_fusion.mine_ref = bf16[4,6,48,384]{3,2,1,0:T(8,128)(2,1)S(1)} fusion(bf16[1,6,48,384]{3,2,1,0:T(8,128)(2,1)} %bitcast.14, bf16[1,6,48,384]{3,2,1,0:T(8,128)(2,1)} %bitcast.13, bf16[1,6,48,384]{3,2,1,0:T(8,128)(2,1)} %bitcast.12, bf16[1,6,48,384]{3,2,1,0:T(8,128)(2,1)} %bitcast.11), kind=kLoop, calls=%fused_computation.22 | loop fusion | flops 1327104 | bytes 1769472 | tf_op jit(solution)/shard_map/stack | solution.py:129
  63.3 1.9 %collective-permute-start.10 = (bf16[4,6,48,384]{3,2,1,0:T(8,128)(2,1)S(1)}, bf16[4,6,48,384]{3,2,1,0:T(8,128)(2,1)S(1)}, u32[]{:S(2)}, u32[]{:S(2)}) collective-permute-start(bf16[4,6,48,384]{3,2,1,0:T(8,128)(2,1)S(1)} %pad_maximum_fusion.mine_ref), channel_id=1, source_target_pairs={{0,32},{32,0},{64,96},{96,64},{128,160},{160,128},{192,224},{224,1... | collective-permute-start | bytes 2654216 | tf_op jit(solution)/shard_map/ppermute | solution.py:130
  65.2 1.8 %fusion.9 = f32[768,384]{1,0:T(8,128)S(1)} fusion(bf16[768,384]{1,0:T(8,128)(2,1)} %convert_element_type.3, bf16[1,3,768,768]{3,2,1,0:T(8,128)(2,1)S(1)} %copy-done.1, s32[]{:T(128)S(6)} %select_n.86), kind=kOutput, calls=%fused_computation.17 | convolution fusion | flops 452984832 | bytes 2949124 | tf_op jit(solution)/shard_map/dot_general | solution.py:139
  67.1 2.3 %collective-permute-start.12 = (bf16[768,384]{1,0:T(8,128)(2,1)}, bf16[768,384]{1,0:T(8,128)(2,1)S(1)}, u32[]{:S(2)}, u32[]{:S(2)}) collective-permute-start(bf16[768,384]{1,0:T(8,128)(2,1)} %collective-permute-done.11), channel_id=1, source_target_pairs={{0,31},{1,2},{2,1},{3,4},{4,3},{5,6},{6,5},{7,8},{8,7},{9,10},{10,... | collective-permute-start | bytes 1769480 | tf_op jit(solution)/shard_map/ppermute | solution.py:122
  69.5 1.9 %collective-permute-start.14 = (bf16[768,384]{1,0:T(8,128)(2,1)}, bf16[768,384]{1,0:T(8,128)(2,1)S(1)}, u32[]{:S(2)}, u32[]{:S(2)}) collective-permute-start(bf16[768,384]{1,0:T(8,128)(2,1)} %collective-permute-done.13), channel_id=1, source_target_pairs={{0,1},{1,0},{2,3},{3,2},{4,5},{5,4},{6,7},{7,6},{8,9},{9,8},{10,11... | collective-permute-start | bytes 1769480 | tf_op jit(solution)/shard_map/ppermute | solution.py:123
  71.4 1.8 %convolution_add_fusion.1 = f32[768,384]{1,0:T(8,128)S(1)} fusion(f32[768,384]{1,0:T(8,128)S(1)} %fusion.9, bf16[768,384]{1,0:T(8,128)(2,1)} %collective-permute-done, bf16[1,3,768,768]{3,2,1,0:T(8,128)(2,1)S(1)} %copy-done.1, s32[]{:T(128)S(6)} %select_n.89), kind=kOutput, calls=%fused_computation.2 | convolution fusion | flops 453279744 | bytes 4128772 | tf_op jit(solution)/shard_map/dot_general | solution.py:140
  73.6 0.8 fusion
  74.4 14.3 %collective-permute-done.12 = bf16[768,384]{1,0:T(8,128)(2,1)S(1)} collective-permute-done((bf16[768,384]{1,0:T(8,128)(2,1)}, bf16[768,384]{1,0:T(8,128)(2,1)S(1)}, u32[]{:S(2)}, u32[]{:S(2)}) %collective-permute-start.12) | collective-permute-done | bytes 589856 | tf_op jit(solution)/shard_map/ppermute | solution.py:122
  88.7 1.9 %collective-permute-start.15 = (bf16[768,384]{1,0:T(8,128)(2,1)S(1)}, bf16[768,384]{1,0:T(8,128)(2,1)S(1)}, u32[]{:S(2)}, u32[]{:S(2)}) collective-permute-start(bf16[768,384]{1,0:T(8,128)(2,1)S(1)} %collective-permute-done.12), channel_id=1, source_target_pairs={{0,1},{1,0},{2,3},{3,2},{4,5},{5,4},{6,7},{7,6},{8,9},{9,8},{10,11... | collective-permute-start | bytes 1769480 | tf_op jit(solution)/shard_map/ppermute | solution.py:124
  91.1 1.6 %convolution_bitcast_fusion.3 = f32[768,384]{1,0:T(8,128)S(1)} fusion(bf16[768,384]{1,0:T(8,128)(2,1)} %convert_element_type.3, bf16[6,384,384]{2,1,0:T(8,128)(2,1)S(1)} %arrange.1), kind=kOutput, calls=%fused_computation.9 | convolution fusion | flops 226492416 | bytes 2064384 | tf_op jit(solution)/shard_map/dot_general | solution.py:81
  92.7 1.6 %convolution_bitcast_fusion.4 = f32[768,384]{1,0:T(8,128)S(1)} fusion(bf16[768,384]{1,0:T(8,128)(2,1)} %collective-permute-done.13, bf16[6,384,384]{2,1,0:T(8,128)(2,1)S(1)} %arrange.1), kind=kOutput, calls=%fused_computation.10 | convolution fusion | flops 226492416 | bytes 2064384 | tf_op jit(solution)/shard_map/dot_general | solution.py:81
  94.9 1.6 %fusion.3 = f32[768,384]{1,0:T(8,128)S(1)} fusion(f32[768,384]{1,0:T(8,128)S(1)} %fusion.6, bf16[768,384]{1,0:T(8,128)(2,1)} %collective-permute-done.11, bf16[6,384,384]{2,1,0:T(8,128)(2,1)S(1)} %arrange.1), kind=kOutput, calls=%fused_computation.8 | convolution fusion | flops 226787328 | bytes 3244032 | tf_op jit(solution)/shard_map/dot_general | solution.py:81
  97.0 8.4 %collective-permute-done.15 = bf16[768,384]{1,0:T(8,128)(2,1)S(1)} collective-permute-done((bf16[768,384]{1,0:T(8,128)(2,1)S(1)}, bf16[768,384]{1,0:T(8,128)(2,1)S(1)}, u32[]{:S(2)}, u32[]{:S(2)}) %collective-permute-start.15) | collective-permute-done | bytes 589856 | tf_op jit(solution)/shard_map/ppermute | solution.py:124
  105.4 1.5 %fusion.1 = f32[768,384]{1,0:T(8,128)} fusion(f32[768,384]{1,0:T(8,128)S(1)} %fusion.2, bf16[768,384]{1,0:T(8,128)(2,1)S(1)} %collective-permute-done.15, bf16[6,384,384]{2,1,0:T(8,128)(2,1)S(1)} %arrange.1), kind=kOutput, calls=%fused_computation.4 | convolution fusion | flops 226787328 | bytes 3244032 | tf_op jit(solution)/shard_map/dot_general | solution.py:81
  (33 shorter events, 2.9 us)
Async XLA Ops:
  0.0 2.0 %copy-start = (bf16[1,3,768,768]{3,2,1,0:T(8,128)(2,1)S(1)}, bf16[1,3,768,768]{3,2,1,0:T(8,128)(2,1)}, u32[]{:S(2)}) copy-start(bf16[1,3,768,768]{3,2,1,0:T(8,128)(2,1)} %tiles_ref.1) | copy-start | bytes 10616836
  2.0 0.7 copy-start.2
  3.6 0.9 collective-permute-start.2
  4.6 27.6 %copy-start.4 = (f32[768,384]{1,0:T(8,128)S(1)}, f32[768,384]{1,0:T(8,128)}, u32[]{:S(2)}) copy-start(f32[768,384]{1,0:T(8,128)} %param.5) | copy-start | bytes 3538948
  4.7 3.5 %collective-permute-start.3 = (bf16[6,48,384]{2,1,0:T(8,128)(2,1)S(1)}, bf16[6,48,384]{2,1,0:T(8,128)(2,1)S(1)}, u32[]{:S(2)}, u32[]{:S(2)}) collective-permute-start(bf16[6,48,384]{2,1,0:T(8,128)(2,1)S(1)} %get-tuple-element.14), channel_id=1, source_target_pairs={{0,256},{16,320},{32,288},{48,352},{1,257},{17,321},{33,289},{49,3... | collective-permute-start | bytes 663560 | tf_op jit(solution)/shard_map/ppermute | solution.py:118
  5.5 2.7 %collective-permute-start.4 = (bf16[6,48,384]{2,1,0:T(8,128)(2,1)S(1)}, bf16[6,48,384]{2,1,0:T(8,128)(2,1)S(1)}, u32[]{:S(2)}, u32[]{:S(2)}) collective-permute-start(bf16[6,48,384]{2,1,0:T(8,128)(2,1)S(1)} %get-tuple-element.12), channel_id=1, source_target_pairs={{0,128},{16,192},{32,160},{48,224},{1,129},{17,193},{33,161},{49,2... | collective-permute-start | bytes 663560 | tf_op jit(solution)/shard_map/ppermute | solution.py:118
  6.2 2.0 %collective-permute-start.5 = (bf16[6,48,384]{2,1,0:T(8,128)(2,1)S(1)}, bf16[6,48,384]{2,1,0:T(8,128)(2,1)S(1)}, u32[]{:S(2)}, u32[]{:S(2)}) collective-permute-start(bf16[6,48,384]{2,1,0:T(8,128)(2,1)S(1)} %get-tuple-element.13), channel_id=1, source_target_pairs={{0,384},{16,448},{32,416},{48,480},{1,385},{17,449},{33,417},{49,4... | collective-permute-start | bytes 663560 | tf_op jit(solution)/shard_map/ppermute | solution.py:118
  6.9 14.2 %collective-permute-start.6 = (bf16[6,48,384]{2,1,0:T(8,128)(2,1)S(1)}, bf16[6,48,384]{2,1,0:T(8,128)(2,1)S(1)}, u32[]{:S(2)}, u32[]{:S(2)}) collective-permute-start(bf16[6,48,384]{2,1,0:T(8,128)(2,1)S(1)} %get-tuple-element.15), channel_id=1, source_target_pairs={{0,0},{16,64},{32,32},{48,96},{1,1},{17,65},{33,33},{49,97},{2,2},... | collective-permute-start | bytes 663560 | tf_op jit(solution)/shard_map/ppermute | solution.py:118
  21.9 31.2 %copy-start.3 = (s32[1,3]{1,0:T(1,128)S(1)}, s32[1,3]{1,0:T(1,128)}, u32[]{:S(2)}) copy-start(s32[1,3]{1,0:T(1,128)} %cols_ref.1) | copy-start | bytes 40
  21.9 29.3 %collective-permute-start.7 = (bf16[6,48,384]{2,1,0:T(8,128)(2,1)}, bf16[6,48,384]{2,1,0:T(8,128)(2,1)}, u32[]{:S(2)}, u32[]{:S(2)}) collective-permute-start(bf16[6,48,384]{2,1,0:T(8,128)(2,1)} %add_add_fusion), channel_id=1, source_target_pairs={{0,384},{32,416},{64,448},{96,480},{128,0},{160,32},{192,64},{224,... | collective-permute-start | bytes 663560 | tf_op jit(solution)/shard_map/ppermute | solution.py:128
  25.3 34.1 %collective-permute-start.8 = (bf16[6,48,384]{2,1,0:T(8,128)(2,1)}, bf16[6,48,384]{2,1,0:T(8,128)(2,1)}, u32[]{:S(2)}, u32[]{:S(2)}) collective-permute-start(bf16[6,48,384]{2,1,0:T(8,128)(2,1)} %add_add_fusion), channel_id=1, source_target_pairs={{0,256},{32,288},{64,320},{96,352},{128,384},{160,416},{192,448},{... | collective-permute-start | bytes 663560 | tf_op jit(solution)/shard_map/ppermute | solution.py:128
  30.2 31.6 %collective-permute-start.9 = (bf16[6,48,384]{2,1,0:T(8,128)(2,1)}, bf16[6,48,384]{2,1,0:T(8,128)(2,1)}, u32[]{:S(2)}, u32[]{:S(2)}) collective-permute-start(bf16[6,48,384]{2,1,0:T(8,128)(2,1)} %add_add_fusion), channel_id=1, source_target_pairs={{0,128},{32,160},{64,192},{96,224},{128,256},{160,288},{192,320},{... | collective-permute-start | bytes 663560 | tf_op jit(solution)/shard_map/ppermute | solution.py:128
  32.2 33.0 %copy-start.1 = (bf16[1,3,768,768]{3,2,1,0:T(8,128)(2,1)S(1)}, bf16[1,3,768,768]{3,2,1,0:T(8,128)(2,1)}, u32[]{:S(2)}) copy-start(bf16[1,3,768,768]{3,2,1,0:T(8,128)(2,1)} %tiles_ref.1) | copy-start | bytes 10616836
  33.1 34.0 %collective-permute-start.11 = (bf16[768,384]{1,0:T(8,128)(2,1)}, bf16[768,384]{1,0:T(8,128)(2,1)}, u32[]{:S(2)}, u32[]{:S(2)}) collective-permute-start(bf16[768,384]{1,0:T(8,128)(2,1)} %convert_element_type.3), channel_id=1, source_target_pairs={{0,1},{1,0},{2,3},{3,2},{4,5},{5,4},{6,7},{7,6},{8,9},{9,8},{10,11... | collective-permute-start | bytes 1769480 | tf_op jit(solution)/shard_map/ppermute | solution.py:107
  37.0 32.4 %collective-permute-start.13 = (bf16[768,384]{1,0:T(8,128)(2,1)}, bf16[768,384]{1,0:T(8,128)(2,1)}, u32[]{:S(2)}, u32[]{:S(2)}) collective-permute-start(bf16[768,384]{1,0:T(8,128)(2,1)} %convert_element_type.3), channel_id=1, source_target_pairs={{0,31},{1,2},{2,1},{3,4},{4,3},{5,6},{6,5},{7,8},{8,7},{9,10},{10,... | collective-permute-start | bytes 1769480 | tf_op jit(solution)/shard_map/ppermute | solution.py:106
  51.2 20.2 %collective-permute-start = (bf16[768,384]{1,0:T(8,128)(2,1)}, bf16[768,384]{1,0:T(8,128)(2,1)}, u32[]{:S(2)}, u32[]{:S(2)}) collective-permute-start(bf16[768,384]{1,0:T(8,128)(2,1)} %convert_element_type.3), channel_id=1, source_target_pairs={{0,480},{32,0},{64,32},{96,64},{128,96},{160,128},{192,160},{224,1... | collective-permute-start | bytes 1769480 | tf_op jit(solution)/shard_map/ppermute | solution.py:120
  59.4 14.2 %collective-permute-start.1 = (bf16[768,384]{1,0:T(8,128)(2,1)}, bf16[768,384]{1,0:T(8,128)(2,1)S(1)}, u32[]{:S(2)}, u32[]{:S(2)}) collective-permute-start(bf16[768,384]{1,0:T(8,128)(2,1)} %convert_element_type.3), channel_id=1, source_target_pairs={{0,32},{32,64},{64,96},{96,128},{128,160},{160,192},{192,224},{224... | collective-permute-start | bytes 1769480 | tf_op jit(solution)/shard_map/ppermute | solution.py:121
  63.3 27.3 %collective-permute-start.10 = (bf16[4,6,48,384]{3,2,1,0:T(8,128)(2,1)S(1)}, bf16[4,6,48,384]{3,2,1,0:T(8,128)(2,1)S(1)}, u32[]{:S(2)}, u32[]{:S(2)}) collective-permute-start(bf16[4,6,48,384]{3,2,1,0:T(8,128)(2,1)S(1)} %pad_maximum_fusion.mine_ref), channel_id=1, source_target_pairs={{0,32},{32,0},{64,96},{96,64},{128,160},{160,128},{192,224},{224,1... | collective-permute-start | bytes 2654216 | tf_op jit(solution)/shard_map/ppermute | solution.py:130
  67.1 6.5 %copy-start.5 = (f32[768,384]{1,0:T(8,128)S(1)}, f32[768,384]{1,0:T(8,128)}, u32[]{:S(2)}) copy-start(f32[768,384]{1,0:T(8,128)} %param.5) | copy-start | bytes 3538948
  67.1 6.5 %copy-start.6 = (f32[768]{0:T(1024)S(1)}, f32[768]{0:T(1024)}, u32[]{:S(2)}) copy-start(f32[768]{0:T(1024)} %param.8) | copy-start | bytes 9220
  67.1 6.5 %copy-start.7 = (f32[384]{0:T(512)S(1)}, f32[384]{0:T(512)}, u32[]{:S(2)}) copy-start(f32[384]{0:T(512)} %param.9) | copy-start | bytes 4612
  67.1 21.6 %collective-permute-start.12 = (bf16[768,384]{1,0:T(8,128)(2,1)}, bf16[768,384]{1,0:T(8,128)(2,1)S(1)}, u32[]{:S(2)}, u32[]{:S(2)}) collective-permute-start(bf16[768,384]{1,0:T(8,128)(2,1)} %collective-permute-done.11), channel_id=1, source_target_pairs={{0,31},{1,2},{2,1},{3,4},{4,3},{5,6},{6,5},{7,8},{8,7},{9,10},{10,... | collective-permute-start | bytes 1769480 | tf_op jit(solution)/shard_map/ppermute | solution.py:122
  69.5 27.0 %collective-permute-start.14 = (bf16[768,384]{1,0:T(8,128)(2,1)}, bf16[768,384]{1,0:T(8,128)(2,1)S(1)}, u32[]{:S(2)}, u32[]{:S(2)}) collective-permute-start(bf16[768,384]{1,0:T(8,128)(2,1)} %collective-permute-done.13), channel_id=1, source_target_pairs={{0,1},{1,0},{2,3},{3,2},{4,5},{5,4},{6,7},{7,6},{8,9},{9,8},{10,11... | collective-permute-start | bytes 1769480 | tf_op jit(solution)/shard_map/ppermute | solution.py:123
  88.7 16.8 %collective-permute-start.15 = (bf16[768,384]{1,0:T(8,128)(2,1)S(1)}, bf16[768,384]{1,0:T(8,128)(2,1)S(1)}, u32[]{:S(2)}, u32[]{:S(2)}) collective-permute-start(bf16[768,384]{1,0:T(8,128)(2,1)S(1)} %collective-permute-done.12), channel_id=1, source_target_pairs={{0,1},{1,0},{2,3},{3,2},{4,5},{5,4},{6,7},{7,6},{8,9},{9,8},{10,11... | collective-permute-start | bytes 1769480 | tf_op jit(solution)/shard_map/ppermute | solution.py:124

commit v2 on v1

v2 whole, which is shorter than its diff:
```python
import jax
import jax.numpy as jnp
from jax import lax
from jax.experimental import pallas as pl
from jax.experimental.pallas import tpu as pltpu
from jax.sharding import PartitionSpec as P


BOTH = ("aa", "ba")
ANY = pl.BlockSpec(memory_space=pl.ANY)
SCALARS = pl.BlockSpec(memory_space=pltpu.SMEM)
IN_HBM = pl.BlockSpec(memory_space=pltpu.HBM)
ON_CHIP = pl.BlockSpec(memory_space=pltpu.VMEM)
SMALL = pltpu.CompilerParams(vmem_limit_bytes=4 * 1024 * 1024)
LARGE = pltpu.CompilerParams(vmem_limit_bytes=20 * 1024 * 1024)


def prepare(tile_cols, tile_values, coefficients):
    rows = lax.axis_size("aa")
    tile = tile_values.shape[2]
    chunk, piece, steps = tile // 2, tile // 16, 3

    def kernel(cols_ref, tiles_ref, full_ref, low_ref, own_ref, other_ref, sems):
        row = lax.axis_index("aa")
        half = lax.rem(lax.axis_index("ba"), 2)
        core, x = lax.rem(row, 2), lax.div(row, 4)

        def copies():
            made = []
            for index, (out_ref, core_of) in enumerate(((other_ref, 1 - core), (own_ref, core))):
                for t in range(6):
                    place = jnp.where(half == 1, 5 - t, t)
                    block = lax.rem(row + lax.div(place, 2) + rows - 1, rows)
                    slot = jnp.where(cols_ref[0, 1] == block, 1, jnp.where(cols_ref[0, 2] == block, 2, 0))
                    side = pl.multiple_of(lax.rem(place, 2) * chunk, 128)
                    for step in range(4):
                        start = half * chunk + (core_of * 4 + lax.rem(x + step, 4)) * piece
                        source = tiles_ref.at[0, slot, pl.ds(pl.multiple_of(start, 16), piece), pl.ds(side, chunk)]
                        sem = sems.at[index * 24 + t * 4 + step]
                        made.append(pltpu.make_async_copy(source, out_ref.at[step, t], sem))
            return made

        @pl.when(pl.program_id(0) == 0)
        def _():
            for each in copies():
                each.start()

        low_ref[...] = full_ref[...].astype(jnp.bfloat16)

        @pl.when(pl.program_id(0) == steps - 1)
        def _():
            for each in copies():
                each.wait()

    shape = jax.ShapeDtypeStruct((4, 6, piece, chunk), jnp.bfloat16)
    block = pl.BlockSpec((tile // steps, chunk), lambda i: (i, 0))
    whole = pl.BlockSpec((4, 6, piece, chunk), lambda i: (0, 0, 0, 0))
    return pl.pallas_call(
        kernel,
        grid=(steps,),
        out_shape=(jax.ShapeDtypeStruct(coefficients.shape, jnp.bfloat16), shape, shape),
        in_specs=[SCALARS, IN_HBM, block],
        out_specs=(block, whole, whole),
        scratch_shapes=[pltpu.SemaphoreType.DMA((48,))],
        name="prepare",
    )(tile_cols, tile_values, coefficients)


def stack(*values):
    counts = [value.shape[0] if value.ndim == 4 else 1 for value in values]

    def kernel(*refs):
        out_ref, sems = refs[-2:]
        copies, at = [], 0
        for index, (ref, count) in enumerate(zip(refs, counts)):
            target = out_ref.at[pl.ds(at, count)] if len(ref.shape) == 4 else out_ref.at[at]
            copies.append(pltpu.make_async_copy(ref, target, sems.at[index]))
            at += count
        for each in copies:
            each.start()
        for each in copies:
            each.wait()

    return pl.pallas_call(
        kernel,
        out_shape=jax.ShapeDtypeStruct((sum(counts),) + values[0].shape[-3:], values[0].dtype),
        in_specs=[ANY] * len(values),
        out_specs=ANY,
        scratch_shapes=[pltpu.SemaphoreType.DMA((len(values),))],
        compiler_params=SMALL,
        name="stack",
    )(*values)


def choose(values):
    def kernel(*refs):
        out_ref, sem = refs[-2:]
        holder_x = lax.div(lax.axis_index("ba"), 8)
        step = lax.rem(lax.div(lax.axis_index("aa"), 4) + 4 - holder_x, 4)
        for index, ref in enumerate(refs[:-2]):

            @pl.when(step == index)
            def _():
                copy = pltpu.make_async_copy(ref, out_ref, sem)
                copy.start()
                copy.wait()

    return pl.pallas_call(
        kernel,
        out_shape=jax.ShapeDtypeStruct(values[0].shape, values[0].dtype),
        in_specs=[ANY] * len(values),
        out_specs=ANY,
        scratch_shapes=[pltpu.SemaphoreType.DMA],
        compiler_params=SMALL,
        name="choose",
    )(*values)


def alpha_part(tile_cols, tile_values, low, outer, swap, coefficients, alpha_energy, beta_energy):
    rows = lax.axis_size("aa")
    tile, chunk = low.shape

    def kernel(
        cols_ref, tiles_ref, low_ref, outer_ref, swap_ref, full_ref, alpha_ref, beta_ref, out_ref,
        rows_ref, value_ref, held_ref, sems, value_sems, held_sem,
    ):
        row = lax.axis_index("aa")
        odd = lax.rem(row, 2)
        loads = []
        for index, (shift_by, ref) in enumerate(((0, low_ref), (odd, outer_ref), (1 - odd, swap_ref))):
            block = lax.rem(row + (rows - 1 + 2 * shift_by if index else 0), rows)
            slot = jnp.where(cols_ref[0, 1] == block, 1, jnp.where(cols_ref[0, 2] == block, 2, 0))
            loads.append((
                pltpu.make_async_copy(ref, value_ref.at[pl.ds(index * tile, tile)], value_sems.at[index]),
                pltpu.make_async_copy(tiles_ref.at[0, slot], rows_ref.at[:, pl.ds(index * tile, tile)], sems.at[index]),
            ))
        last = pltpu.make_async_copy(full_ref, held_ref, held_sem)
        for pair in loads:
            for each in pair:
                each.start()
        last.start()
        for pair in loads:
            for each in pair:
                each.wait()
        last.wait()
        energy = (alpha_ref[...] + beta_ref[...]) * held_ref[...]
        out_ref[...] = energy + jnp.dot(rows_ref[...], value_ref[...], preferred_element_type=jnp.float32)

    return pl.pallas_call(
        kernel,
        out_shape=jax.ShapeDtypeStruct((tile, chunk), jnp.float32),
        in_specs=[SCALARS, IN_HBM, ANY, ANY, ANY, IN_HBM, ON_CHIP, ON_CHIP],
        out_specs=ON_CHIP,
        scratch_shapes=[
            pltpu.VMEM((tile, 3 * tile), jnp.bfloat16),
            pltpu.VMEM((3 * tile, chunk), jnp.bfloat16),
            pltpu.VMEM((tile, chunk), jnp.float32),
            pltpu.SemaphoreType.DMA((3,)),
            pltpu.SemaphoreType.DMA((3,)),
            pltpu.SemaphoreType.DMA,
        ],
        compiler_params=LARGE,
        name="alpha_part",
    )(tile_cols, tile_values, low, outer, swap, coefficients, alpha_energy[:, None], beta_energy[None, :])


def beta_part(total, mine, theirs, values):
    tile, chunk = total.shape
    count, parts, piece, _ = mine.shape
    known = len(values)

    def kernel(*refs):
        total_ref, mine_ref, theirs_ref = refs[:3]
        value_refs = refs[3 : 3 + known]
        out_ref, last_ref, weight_ref, value_ref, sems, value_sems, last_sem = refs[3 + known :]
        place = lax.axis_index("aa")
        x, core = lax.div(place, 4), lax.rem(place, 2)
        swapped = x + 1 - 2 * lax.rem(x, 2)
        copies = []
        for index, (source, core_of) in enumerate(((mine_ref, core), (theirs_ref, 1 - core))):
            for step, x_of in enumerate((x, swapped, 3 - x, 3 - swapped)):
                at = pl.multiple_of((core_of * count + x_of) * piece, 16)
                for t in range(parts):
                    target = weight_ref.at[pl.ds(at, piece), pl.ds(t * chunk, chunk)]
                    sem = sems.at[(index * count + step) * parts + t]
                    copies.append(pltpu.make_async_copy(source.at[step, t], target, sem))
        for index, ref in enumerate(value_refs):
            target = value_ref.at[:, pl.ds(index * chunk, chunk)]
            copies.append(pltpu.make_async_copy(ref, target, value_sems.at[index]))
        for each in copies:
            each.start()
        for each in copies:
            each.wait()
        last = pltpu.make_async_copy(weight_ref.at[:, pl.ds(known * chunk, chunk)], last_ref, last_sem)
        last.start()
        out_ref[...] = total_ref[...] + times(value_ref[...], weight_ref[:, : known * chunk])
        last.wait()

    return pl.pallas_call(
        kernel,
        out_shape=(
            jax.ShapeDtypeStruct((tile, chunk), jnp.float32),
            jax.ShapeDtypeStruct((chunk, chunk), jnp.bfloat16),
        ),
        in_specs=[ON_CHIP, ANY, ANY] + [ANY] * known,
        out_specs=(ON_CHIP, ANY),
        scratch_shapes=[
            pltpu.VMEM((chunk, parts * chunk), jnp.bfloat16),
            pltpu.VMEM((tile, known * chunk), jnp.bfloat16),
            pltpu.SemaphoreType.DMA((2 * count * parts,)),
            pltpu.SemaphoreType.DMA((known,)),
            pltpu.SemaphoreType.DMA,
        ],
        compiler_params=LARGE,
        name="beta_part",
    )(total, mine, theirs, *values)


def times(left, right):
    return lax.dot_general(left, right, (((1,), (1,)), ((), ())), preferred_element_type=jnp.float32)


def spread_pairs(step, cols):
    pairs = []
    for b in range(cols):
        row, upper, depth = b // 2, b // 16, b % 16
        for core in range(2):
            for y in range(2):
                x_of, y_of = row // 4, (row // 2) % 2
                source_upper = upper if y == y_of else 1 - upper
                source = (x_of * 4 + y_of * 2 + core) * cols + source_upper * 16 + depth
                target = (((x_of + step) % 4) * 4 + y * 2 + core) * cols + b
                pairs.append((source, target))
    return pairs


def body(coefficients, tile_values, tile_cols, alpha_energy, beta_energy):
    rows, cols = lax.axis_size("aa"), lax.axis_size("ba")
    a, depth = lax.axis_index("aa"), lax.axis_index("ba") % 16
    across = [(j, (j + 1) % cols if j % 2 else (j - 1) % cols) for j in range(cols)]
    within = [(j, j ^ 1) for j in range(cols)]

    low, own_half, other_half = prepare(tile_cols, tile_values, coefficients)
    near = lax.ppermute(low, "ba", across)
    sibling = lax.ppermute(low, "ba", within)

    holders = [
        (i * cols + j, (i ^ 1) * cols + j) for i in range(rows) for j in range(cols) if i % 8 == (j % 16) // 2
    ]
    passed = lax.ppermute(other_half, BOTH, holders)
    held = jnp.where(a % 8 == depth // 2, own_half, passed)
    spread = [lax.ppermute(held[step], BOTH, spread_pairs(step, cols)) for step in range(4)]
    got = choose(spread)

    outer = lax.ppermute(low, "aa", [(i, (i + 1) % rows if i % 2 else (i - 1) % rows) for i in range(rows)])
    swap = lax.ppermute(low, "aa", [(i, i ^ 1) for i in range(rows)])
    far = lax.ppermute(sibling, "ba", across)
    next_near = lax.ppermute(near, "ba", within)
    next_far = lax.ppermute(far, "ba", within)

    pair = stack(got, lax.ppermute(got, "aa", [(i, i ^ 4) for i in range(rows)]))
    mine = stack(pair, lax.ppermute(pair, "aa", [(i, i ^ 12) for i in range(rows)]))
    theirs = lax.ppermute(mine, "aa", [(i, i ^ 1) for i in range(rows)])

    total = alpha_part(tile_cols, tile_values, low, outer, swap, coefficients, alpha_energy, beta_energy)
    total, last = beta_part(total, mine, theirs, (far, near, low, sibling, next_near))
    return total + times(next_far, last)


def solution(mesh):
    in_specs = (P("aa", "ba"), P("aa", None, None, None), P("aa", None), P("aa"), P("ba"))
    out_specs = P("aa", "ba")
    return jax.shard_map(body, mesh=mesh, in_specs=in_specs, out_specs=out_specs, check_vma=False)
```

time: 108 us -> 105 us (0.972)
  Pallas kernels: 1.45 us -> 12.5 us
  matrix products: 11.9 us -> 1.54 us
  starting transfers between devices: 44.9 us -> 52.2 us
  between operations: 6.13 us -> 0.37 us
  other arithmetic: 3.85 us -> 0.12 us
  local copies, waits for them, and re-layouts: 2.81 us -> 0.29 us
    pallas_call x2 -> x6, Pallas kernels: 1.45 us -> 12.5 us  [the longest x1 4.66 us: prepare(): pl.pallas_call(kernel, grid=(steps,), out_shape=(jax.ShapeDtypeStruct(coe...]
    ppermute x1, waiting for transfers between devices: 0.01 us -> 8.97 us  [body(): near = lax.ppermute(low, 'ba', across)]
    dot_general x6 -> x1, matrix products: 7.4 us -> 1.54 us  [times(): lax.dot_general(left, right, (((1,), (1,)), ((), ())), preferred_element_...]
    dot_general x3 -> x0, matrix products: 4.46 us -> none  [the longest x1 1.84 us: body(): jnp.dot(tile_of((a + 1) % rows), above, preferred_element_type=jnp.float32)]
    ppermute x1, starting transfers between devices: 14.2 us -> 18.3 us  [body(): near = lax.ppermute(low, 'ba', across)]
    ppermute x9 -> x8, starting transfers between devices: 18 us -> 21.7 us  [the longest x1 7.64 us: body(): lax.ppermute(pair, 'aa', [(i, i ^ 12) for i in range(rows)])]
    ppermute x1, waiting for transfers between devices: 8.41 us -> 5.09 us  [body(): next_far = lax.ppermute(far, 'ba', within)]
    unnamed x16 -> x12, local copies, waits for them, and re-layouts: 2.69 us -> 0.04 us
  transfers between devices with their start and end apart: 16 -> 15, of which waited for: 4 -> 6; matrix products, arithmetic and copies ran while one was open for 12% -> 0% of each run, Pallas kernels for 0% -> 8%
where the time goes in v2:
time: 105 us; the launch traced here: 104 us
  starting transfers between devices  52.2 us (50%)
  waiting for transfers between devices  37 us (35%)
  Pallas kernels  12.5 us (12%)
  matrix products  1.54 us (1%)
    ppermute x1, starting transfers between devices, body(): near = lax.ppermute(low, 'ba', across)  18.3 us
    ppermute x1, waiting for transfers between devices, body(): far = lax.ppermute(sibling, 'ba', across)  12.2 us
    ppermute x1, waiting for transfers between devices, body(): near = lax.ppermute(low, 'ba', across)  8.97 us
    ppermute x1, starting transfers between devices, body(): lax.ppermute(pair, 'aa', [(i, i ^ 12) for i in range(rows)])  7.64 us
    ppermute x1, starting transfers between devices, body(): lax.ppermute(got, 'aa', [(i, i ^ 4) for i in range(rows)])  6.28 us
    ppermute x1, waiting for transfers between devices, body(): next_far = lax.ppermute(far, 'ba', within)  5.09 us
    ppermute x4, waiting for transfers between devices, body(): lax.ppermute(held[step], BOTH, spread_pairs(step, cols))  4.84 us
    pallas_call x1, Pallas kernels, prepare(): pl.pallas_call(kernel, grid=(steps,), out_shape=(jax.ShapeDtypeStruct(coe...  4.66 us
  transfers between devices with their start and end apart: 15, of which 6 were waited for; matrix products, arithmetic and copies ran while one was open for 0% of the time, Pallas kernels for 8%

profile of v2, /device:TPU:8, one launch (start us, length us, event | category | flops | bytes accessed | tf_op | source)
XLA Modules:
  0.0 104.1 jit_solution(5431364598913556343)
XLA Ops:
  0.0 4.7 %prepare.1 = (bf16[768,384]{1,0:T(8,128)(2,1)}, bf16[4,6,48,384]{3,2,1,0:T(8,128)(2,1)}, bf16[4,6,48,384]{3,2,1,0:T(8,128)(2,1)}) custom-call(s32[1,3]{1,0:T(1,128)} %cols_ref.3, bf16[1,3,768,768]{3,2,1,0:T(8,128)(2,1)} %tiles_ref.3, f32[768,384]{1,0:T(8,128)} %full_ref.3), custom_call_target="tpu_custom_call" | custom-call | tf_op jit(solution)/shard_map/prepare/pallas_call | solution.py:58
  4.7 0.7 collective-permute-start.2
  5.4 0.1 broadcast_select_fusion
  5.6 0.0 copy-start.1
  5.6 0.1 slice_bitcast_fusion
  5.7 1.4 %collective-permute-start.3 = (bf16[6,48,384]{2,1,0:T(8,128)(2,1)S(1)}, bf16[6,48,384]{2,1,0:T(8,128)(2,1)S(1)}, u32[]{:S(2)}, u32[]{:S(2)}) collective-permute-start(bf16[6,48,384]{2,1,0:T(8,128)(2,1)S(1)} %get-tuple-element.18), channel_id=1, source_target_pairs={{0,0},{16,64},{32,32},{48,96},{1,1},{17,65},{33,33},{49,97},{2,2},... | collective-permute-start | bytes 663560 | tf_op jit(solution)/shard_map/ppermute | solution.py:252
  7.1 0.7 collective-permute-start.4
  7.8 0.7 collective-permute-start.5
  8.5 0.7 collective-permute-start.6
  9.2 3.8 %collective-permute-start.10 = (bf16[768,384]{1,0:T(8,128)(2,1)S(1)}, bf16[768,384]{1,0:T(8,128)(2,1)S(1)}, u32[]{:S(2)}, u32[]{:S(2)}) collective-permute-start(bf16[768,384]{1,0:T(8,128)(2,1)S(1)} %copy-done.2), channel_id=1, source_target_pairs={{0,1},{1,0},{2,3},{3,2},{4,5},{5,4},{6,7},{7,6},{8,9},{9,8},{10,11... | collective-permute-start | bytes 1769480 | tf_op jit(solution)/shard_map/ppermute | solution.py:245
  13.0 4.8 %collective-permute-done.3.refs_0_ = bf16[6,48,384]{2,1,0:T(8,128)(2,1)S(1)} collective-permute-done((bf16[6,48,384]{2,1,0:T(8,128)(2,1)S(1)}, bf16[6,48,384]{2,1,0:T(8,128)(2,1)S(1)}, u32[]{:S(2)}, u32[]{:S(2)}) %collective-permute-start.3) | collective-permute-done | bytes 221216 | tf_op jit(solution)/shard_map/ppermute | solution.py:252
  17.9 0.3 choose.1.refs_0_
  18.2 6.3 %collective-permute-start.7 = (bf16[6,48,384]{2,1,0:T(8,128)(2,1)S(1)}, bf16[6,48,384]{2,1,0:T(8,128)(2,1)S(1)}, u32[]{:S(2)}, u32[]{:S(2)}) collective-permute-start(bf16[6,48,384]{2,1,0:T(8,128)(2,1)S(1)} %choose.1.refs_0_), channel_id=1, source_target_pairs={{0,128},{32,160},{64,192},{96,224},{128,0},{160,32},{192,64},{224,... | collective-permute-start | bytes 663560 | tf_op jit(solution)/shard_map/ppermute | solution.py:261
  24.5 3.9 %collective-permute-done.7.refs_1_ = bf16[6,48,384]{2,1,0:T(8,128)(2,1)S(1)} collective-permute-done((bf16[6,48,384]{2,1,0:T(8,128)(2,1)S(1)}, bf16[6,48,384]{2,1,0:T(8,128)(2,1)S(1)}, u32[]{:S(2)}, u32[]{:S(2)}) %collective-permute-start.7) | collective-permute-done | bytes 221216 | tf_op jit(solution)/shard_map/ppermute | solution.py:261
  28.4 0.6 stack.2.refs_0_
  29.0 7.6 %collective-permute-start.8 = (bf16[2,6,48,384]{3,2,1,0:T(8,128)(2,1)S(1)}, bf16[2,6,48,384]{3,2,1,0:T(8,128)(2,1)S(1)}, u32[]{:S(2)}, u32[]{:S(2)}) collective-permute-start(bf16[2,6,48,384]{3,2,1,0:T(8,128)(2,1)S(1)} %stack.2.refs_0_), channel_id=1, source_target_pairs={{0,384},{32,416},{64,448},{96,480},{128,256},{160,288},{192,320},{... | collective-permute-start | bytes 1327112 | tf_op jit(solution)/shard_map/ppermute | solution.py:262
  36.6 18.3 %collective-permute-start.12 = (bf16[768,384]{1,0:T(8,128)(2,1)S(1)}, bf16[768,384]{1,0:T(8,128)(2,1)S(1)}, u32[]{:S(2)}, u32[]{:S(2)}) collective-permute-start(bf16[768,384]{1,0:T(8,128)(2,1)S(1)} %copy-done.2), channel_id=1, source_target_pairs={{0,31},{1,2},{2,1},{3,4},{4,3},{5,6},{6,5},{7,8},{8,7},{9,10},{10,... | collective-permute-start | bytes 1769480 | tf_op jit(solution)/shard_map/ppermute | solution.py:244
  55.0 1.9 %collective-permute-start.11 = (bf16[768,384]{1,0:T(8,128)(2,1)S(1)}, bf16[768,384]{1,0:T(8,128)(2,1)S(1)}, u32[]{:S(2)}, u32[]{:S(2)}) collective-permute-start(bf16[768,384]{1,0:T(8,128)(2,1)S(1)} %collective-permute-done.10.refs_6_), channel_id=1, source_target_pairs={{0,31},{1,2},{2,1},{3,4},{4,3},{5,6},{6,5},{7,8},{8,7},{9,10},{10,... | collective-permute-start | bytes 1769480 | tf_op jit(solution)/shard_map/ppermute | solution.py:257
  56.9 0.5 stack.3.refs_1_
  57.4 1.9 %collective-permute-start.9 = (bf16[4,6,48,384]{3,2,1,0:T(8,128)(2,1)S(1)}, bf16[4,6,48,384]{3,2,1,0:T(8,128)(2,1)S(1)}, u32[]{:S(2)}, u32[]{:S(2)}) collective-permute-start(bf16[4,6,48,384]{3,2,1,0:T(8,128)(2,1)S(1)} %stack.3.refs_1_), channel_id=1, source_target_pairs={{0,32},{32,0},{64,96},{96,64},{128,160},{160,128},{192,224},{224,1... | collective-permute-start | bytes 2654216 | tf_op jit(solution)/shard_map/ppermute | solution.py:263
  59.4 1.9 %collective-permute-start = (bf16[768,384]{1,0:T(8,128)(2,1)S(1)}, bf16[768,384]{1,0:T(8,128)(2,1)S(1)}, u32[]{:S(2)}, u32[]{:S(2)}) collective-permute-start(bf16[768,384]{1,0:T(8,128)(2,1)S(1)} %copy-done.2), channel_id=1, source_target_pairs={{0,480},{32,64},{64,32},{96,128},{128,96},{160,192},{192,160},{224... | collective-permute-start | bytes 1769480 | tf_op jit(solution)/shard_map/ppermute | solution.py:255
  61.3 2.4 %collective-permute-start.1 = (bf16[768,384]{1,0:T(8,128)(2,1)S(1)}, bf16[768,384]{1,0:T(8,128)(2,1)S(1)}, u32[]{:S(2)}, u32[]{:S(2)}) collective-permute-start(bf16[768,384]{1,0:T(8,128)(2,1)S(1)} %copy-done.2), channel_id=1, source_target_pairs={{0,32},{32,0},{64,96},{96,64},{128,160},{160,128},{192,224},{224,1... | collective-permute-start | bytes 1769480 | tf_op jit(solution)/shard_map/ppermute | solution.py:256
  63.7 9.0 %collective-permute-done.12.refs_4_ = bf16[768,384]{1,0:T(8,128)(2,1)S(1)} collective-permute-done((bf16[768,384]{1,0:T(8,128)(2,1)S(1)}, bf16[768,384]{1,0:T(8,128)(2,1)S(1)}, u32[]{:S(2)}, u32[]{:S(2)}) %collective-permute-start.12) | collective-permute-done | bytes 589856 | tf_op jit(solution)/shard_map/ppermute | solution.py:244
  72.7 1.9 %collective-permute-start.13 = (bf16[768,384]{1,0:T(8,128)(2,1)S(1)}, bf16[768,384]{1,0:T(8,128)(2,1)S(1)}, u32[]{:S(2)}, u32[]{:S(2)}) collective-permute-start(bf16[768,384]{1,0:T(8,128)(2,1)S(1)} %collective-permute-done.12.refs_4_), channel_id=1, source_target_pairs={{0,1},{1,0},{2,3},{3,2},{4,5},{5,4},{6,7},{7,6},{8,9},{9,8},{10,11... | collective-permute-start | bytes 1769480 | tf_op jit(solution)/shard_map/ppermute | solution.py:258
  74.6 12.2 %collective-permute-done.11.refs_3_ = bf16[768,384]{1,0:T(8,128)(2,1)S(1)} collective-permute-done((bf16[768,384]{1,0:T(8,128)(2,1)S(1)}, bf16[768,384]{1,0:T(8,128)(2,1)S(1)}, u32[]{:S(2)}, u32[]{:S(2)}) %collective-permute-start.11) | collective-permute-done | bytes 589856 | tf_op jit(solution)/shard_map/ppermute | solution.py:257
  86.8 1.9 %collective-permute-start.14 = (bf16[768,384]{1,0:T(8,128)(2,1)S(1)}, bf16[768,384]{1,0:T(8,128)(2,1)S(1)}, u32[]{:S(2)}, u32[]{:S(2)}) collective-permute-start(bf16[768,384]{1,0:T(8,128)(2,1)S(1)} %collective-permute-done.11.refs_3_), channel_id=1, source_target_pairs={{0,1},{1,0},{2,3},{3,2},{4,5},{5,4},{6,7},{7,6},{8,9},{9,8},{10,11... | collective-permute-start | bytes 1769480 | tf_op jit(solution)/shard_map/ppermute | solution.py:259
  88.7 0.2 broadcast_in_dim.8.alpha_ref
  88.9 2.1 %collective-permute-done.outer_ref = bf16[768,384]{1,0:T(8,128)(2,1)S(1)} collective-permute-done((bf16[768,384]{1,0:T(8,128)(2,1)S(1)}, bf16[768,384]{1,0:T(8,128)(2,1)S(1)}, u32[]{:S(2)}, u32[]{:S(2)}) %collective-permute-start) | collective-permute-done | bytes 589856 | tf_op jit(solution)/shard_map/ppermute | solution.py:255
  91.0 3.5 %alpha_part.1.refs_0_ = f32[768,384]{1,0:T(8,128)S(1)} custom-call(s32[1,3]{1,0:T(1,128)S(1)} %copy-done.3, bf16[1,3,768,768]{3,2,1,0:T(8,128)(2,1)S(1)} %copy-done, bf16[768,384]{1,0:T(8,128)(2,1)S(1)} %copy-done.2, bf16[768,384]{1,0:T(8,128)(2,1)S(1)} %collective-permute-done.outer_ref, bf16[768,384]{1,0:T(8,128)(2,1)S(1)} %collective-permute-done.1.swap_ref, ...), custom_call_target="tpu_custom_call" | custom-call | tf_op jit(solution)/shard_map/alpha_part/pallas_call | solution.py:149
  94.5 3.0 %beta_part.1 = (f32[768,384]{1,0:T(8,128)S(1)}, bf16[384,384]{1,0:T(8,128)(2,1)S(1)}) custom-call(f32[768,384]{1,0:T(8,128)S(1)} %alpha_part.1.refs_0_, bf16[4,6,48,384]{3,2,1,0:T(8,128)(2,1)S(1)} %stack.3.refs_1_, bf16[4,6,48,384]{3,2,1,0:T(8,128)(2,1)S(1)} %collective-permute-done.9.refs_2_, bf16[768,384]{1,0:T(8,128)(2,1)S(1)} %collective-permute-done.11.refs_3_, ...), custom_call_target="tpu_custom_call" | custom-call | tf_op jit(solution)/shard_map/beta_part/pallas_call | solution.py:199
  97.5 5.1 %collective-permute-done.14 = bf16[768,384]{1,0:T(8,128)(2,1)S(1)} collective-permute-done((bf16[768,384]{1,0:T(8,128)(2,1)S(1)}, bf16[768,384]{1,0:T(8,128)(2,1)S(1)}, u32[]{:S(2)}, u32[]{:S(2)}) %collective-permute-start.14) | collective-permute-done | bytes 589856 | tf_op jit(solution)/shard_map/ppermute | solution.py:259
  102.6 1.5 %convolution_add_fusion = f32[768,384]{1,0:T(8,128)} fusion(f32[768,384]{1,0:T(8,128)S(1)} %get-tuple-element.13, bf16[768,384]{1,0:T(8,128)(2,1)S(1)} %collective-permute-done.14, bf16[384,384]{1,0:T(8,128)(2,1)S(1)} %get-tuple-element.14), kind=kOutput, calls=%fused_computation | convolution fusion | flops 226787328 | bytes 3244032 | tf_op jit(solution)/shard_map/dot_general | solution.py:220
  (21 shorter events, 0.1 us)
Async XLA Ops:
  4.7 0.8 collective-permute-start.2
  5.6 3.6 %copy-start.2 = (bf16[768,384]{1,0:T(8,128)(2,1)S(1)}, bf16[768,384]{1,0:T(8,128)(2,1)}, u32[]{:S(2)}) copy-start(bf16[768,384]{1,0:T(8,128)(2,1)} %get-tuple-element.10.low_ref.refs_5_) | copy-start | bytes 1769476
  5.6 85.4 %copy-start.1 = (f32[768,384]{1,0:T(8,128)S(1)}, f32[768,384]{1,0:T(8,128)}, u32[]{:S(2)}) copy-start(f32[768,384]{1,0:T(8,128)} %full_ref.3) | copy-start | bytes 3538948
  5.7 12.2 %collective-permute-start.3 = (bf16[6,48,384]{2,1,0:T(8,128)(2,1)S(1)}, bf16[6,48,384]{2,1,0:T(8,128)(2,1)S(1)}, u32[]{:S(2)}, u32[]{:S(2)}) collective-permute-start(bf16[6,48,384]{2,1,0:T(8,128)(2,1)S(1)} %get-tuple-element.18), channel_id=1, source_target_pairs={{0,0},{16,64},{32,32},{48,96},{1,1},{17,65},{33,33},{49,97},{2,2},... | collective-permute-start | bytes 663560 | tf_op jit(solution)/shard_map/ppermute | solution.py:252
  7.1 10.7 %collective-permute-start.4 = (bf16[6,48,384]{2,1,0:T(8,128)(2,1)S(1)}, bf16[6,48,384]{2,1,0:T(8,128)(2,1)S(1)}, u32[]{:S(2)}, u32[]{:S(2)}) collective-permute-start(bf16[6,48,384]{2,1,0:T(8,128)(2,1)S(1)} %get-tuple-element.17), channel_id=1, source_target_pairs={{0,128},{16,192},{32,160},{48,224},{1,129},{17,193},{33,161},{49,2... | collective-permute-start | bytes 663560 | tf_op jit(solution)/shard_map/ppermute | solution.py:252
  7.8 10.0 %collective-permute-start.5 = (bf16[6,48,384]{2,1,0:T(8,128)(2,1)S(1)}, bf16[6,48,384]{2,1,0:T(8,128)(2,1)S(1)}, u32[]{:S(2)}, u32[]{:S(2)}) collective-permute-start(bf16[6,48,384]{2,1,0:T(8,128)(2,1)S(1)} %get-tuple-element.16), channel_id=1, source_target_pairs={{0,256},{16,320},{32,288},{48,352},{1,257},{17,321},{33,289},{49,3... | collective-permute-start | bytes 663560 | tf_op jit(solution)/shard_map/ppermute | solution.py:252
  8.5 9.4 %collective-permute-start.6 = (bf16[6,48,384]{2,1,0:T(8,128)(2,1)S(1)}, bf16[6,48,384]{2,1,0:T(8,128)(2,1)S(1)}, u32[]{:S(2)}, u32[]{:S(2)}) collective-permute-start(bf16[6,48,384]{2,1,0:T(8,128)(2,1)S(1)} %get-tuple-element.15), channel_id=1, source_target_pairs={{0,384},{16,448},{32,416},{48,480},{1,385},{17,449},{33,417},{49,4... | collective-permute-start | bytes 663560 | tf_op jit(solution)/shard_map/ppermute | solution.py:252
  9.2 45.8 %collective-permute-start.10 = (bf16[768,384]{1,0:T(8,128)(2,1)S(1)}, bf16[768,384]{1,0:T(8,128)(2,1)S(1)}, u32[]{:S(2)}, u32[]{:S(2)}) collective-permute-start(bf16[768,384]{1,0:T(8,128)(2,1)S(1)} %copy-done.2), channel_id=1, source_target_pairs={{0,1},{1,0},{2,3},{3,2},{4,5},{5,4},{6,7},{7,6},{8,9},{9,8},{10,11... | collective-permute-start | bytes 1769480 | tf_op jit(solution)/shard_map/ppermute | solution.py:245
  17.9 73.1 %copy-start = (bf16[1,3,768,768]{3,2,1,0:T(8,128)(2,1)S(1)}, bf16[1,3,768,768]{3,2,1,0:T(8,128)(2,1)}, u32[]{:S(2)}) copy-start(bf16[1,3,768,768]{3,2,1,0:T(8,128)(2,1)} %tiles_ref.3) | copy-start | bytes 10616836
  18.2 70.5 %copy-start.4 = (f32[768]{0:T(1024)S(1)}, f32[768]{0:T(1024)}, u32[]{:S(2)}) copy-start(f32[768]{0:T(1024)} %param.8) | copy-start | bytes 9220
  18.2 10.2 %collective-permute-start.7 = (bf16[6,48,384]{2,1,0:T(8,128)(2,1)S(1)}, bf16[6,48,384]{2,1,0:T(8,128)(2,1)S(1)}, u32[]{:S(2)}, u32[]{:S(2)}) collective-permute-start(bf16[6,48,384]{2,1,0:T(8,128)(2,1)S(1)} %choose.1.refs_0_), channel_id=1, source_target_pairs={{0,128},{32,160},{64,192},{96,224},{128,0},{160,32},{192,64},{224,... | collective-permute-start | bytes 663560 | tf_op jit(solution)/shard_map/ppermute | solution.py:261
  29.0 59.9 %copy-start.5 = (f32[384]{0:T(512)S(1)}, f32[384]{0:T(512)}, u32[]{:S(2)}) copy-start(f32[384]{0:T(512)} %param.9) | copy-start | bytes 4612
  29.0 62.0 %copy-start.3 = (s32[1,3]{1,0:T(1,128)S(1)}, s32[1,3]{1,0:T(1,128)}, u32[]{:S(2)}) copy-start(s32[1,3]{1,0:T(1,128)} %cols_ref.3) | copy-start | bytes 40
  29.0 27.9 %collective-permute-start.8 = (bf16[2,6,48,384]{3,2,1,0:T(8,128)(2,1)S(1)}, bf16[2,6,48,384]{3,2,1,0:T(8,128)(2,1)S(1)}, u32[]{:S(2)}, u32[]{:S(2)}) collective-permute-start(bf16[2,6,48,384]{3,2,1,0:T(8,128)(2,1)S(1)} %stack.2.refs_0_), channel_id=1, source_target_pairs={{0,384},{32,416},{64,448},{96,480},{128,256},{160,288},{192,320},{... | collective-permute-start | bytes 1327112 | tf_op jit(solution)/shard_map/ppermute | solution.py:262
  36.6 36.0 %collective-permute-start.12 = (bf16[768,384]{1,0:T(8,128)(2,1)S(1)}, bf16[768,384]{1,0:T(8,128)(2,1)S(1)}, u32[]{:S(2)}, u32[]{:S(2)}) collective-permute-start(bf16[768,384]{1,0:T(8,128)(2,1)S(1)} %copy-done.2), channel_id=1, source_target_pairs={{0,31},{1,2},{2,1},{3,4},{4,3},{5,6},{6,5},{7,8},{8,7},{9,10},{10,... | collective-permute-start | bytes 1769480 | tf_op jit(solution)/shard_map/ppermute | solution.py:244
  55.0 31.8 %collective-permute-start.11 = (bf16[768,384]{1,0:T(8,128)(2,1)S(1)}, bf16[768,384]{1,0:T(8,128)(2,1)S(1)}, u32[]{:S(2)}, u32[]{:S(2)}) collective-permute-start(bf16[768,384]{1,0:T(8,128)(2,1)S(1)} %collective-permute-done.10.refs_6_), channel_id=1, source_target_pairs={{0,31},{1,2},{2,1},{3,4},{4,3},{5,6},{6,5},{7,8},{8,7},{9,10},{10,... | collective-permute-start | bytes 1769480 | tf_op jit(solution)/shard_map/ppermute | solution.py:257
  57.4 37.0 %collective-permute-start.9 = (bf16[4,6,48,384]{3,2,1,0:T(8,128)(2,1)S(1)}, bf16[4,6,48,384]{3,2,1,0:T(8,128)(2,1)S(1)}, u32[]{:S(2)}, u32[]{:S(2)}) collective-permute-start(bf16[4,6,48,384]{3,2,1,0:T(8,128)(2,1)S(1)} %stack.3.refs_1_), channel_id=1, source_target_pairs={{0,32},{32,0},{64,96},{96,64},{128,160},{160,128},{192,224},{224,1... | collective-permute-start | bytes 2654216 | tf_op jit(solution)/shard_map/ppermute | solution.py:263
  59.4 31.6 %collective-permute-start = (bf16[768,384]{1,0:T(8,128)(2,1)S(1)}, bf16[768,384]{1,0:T(8,128)(2,1)S(1)}, u32[]{:S(2)}, u32[]{:S(2)}) collective-permute-start(bf16[768,384]{1,0:T(8,128)(2,1)S(1)} %copy-done.2), channel_id=1, source_target_pairs={{0,480},{32,64},{64,32},{96,128},{128,96},{160,192},{192,160},{224... | collective-permute-start | bytes 1769480 | tf_op jit(solution)/shard_map/ppermute | solution.py:255
  61.3 29.7 %collective-permute-start.1 = (bf16[768,384]{1,0:T(8,128)(2,1)S(1)}, bf16[768,384]{1,0:T(8,128)(2,1)S(1)}, u32[]{:S(2)}, u32[]{:S(2)}) collective-permute-start(bf16[768,384]{1,0:T(8,128)(2,1)S(1)} %copy-done.2), channel_id=1, source_target_pairs={{0,32},{32,0},{64,96},{96,64},{128,160},{160,128},{192,224},{224,1... | collective-permute-start | bytes 1769480 | tf_op jit(solution)/shard_map/ppermute | solution.py:256
  72.7 21.8 %collective-permute-start.13 = (bf16[768,384]{1,0:T(8,128)(2,1)S(1)}, bf16[768,384]{1,0:T(8,128)(2,1)S(1)}, u32[]{:S(2)}, u32[]{:S(2)}) collective-permute-start(bf16[768,384]{1,0:T(8,128)(2,1)S(1)} %collective-permute-done.12.refs_4_), channel_id=1, source_target_pairs={{0,1},{1,0},{2,3},{3,2},{4,5},{5,4},{6,7},{7,6},{8,9},{9,8},{10,11... | collective-permute-start | bytes 1769480 | tf_op jit(solution)/shard_map/ppermute | solution.py:258
  86.8 15.8 %collective-permute-start.14 = (bf16[768,384]{1,0:T(8,128)(2,1)S(1)}, bf16[768,384]{1,0:T(8,128)(2,1)S(1)}, u32[]{:S(2)}, u32[]{:S(2)}) collective-permute-start(bf16[768,384]{1,0:T(8,128)(2,1)S(1)} %collective-permute-done.11.refs_3_), channel_id=1, source_target_pairs={{0,1},{1,0},{2,3},{3,2},{4,5},{5,4},{6,7},{7,6},{8,9},{9,8},{10,11... | collective-permute-start | bytes 1769480 | tf_op jit(solution)/shard_map/ppermute | solution.py:259

commit v3 on v2

--- a/solution.py
+++ b/solution.py
@@ -40,14 +40,16 @@
                         made.append(pltpu.make_async_copy(source, out_ref.at[step, t], sem))
             return made
 
-        @pl.when(pl.program_id(0) == 0)
+        holds = lax.rem(row, 8) == lax.div(lax.rem(lax.axis_index("ba"), 16), 2)
+
+        @pl.when(holds & (pl.program_id(0) == 0))
         def _():
             for each in copies():
                 each.start()
 
         low_ref[...] = full_ref[...].astype(jnp.bfloat16)
 
-        @pl.when(pl.program_id(0) == steps - 1)
+        @pl.when(holds & (pl.program_id(0) == steps - 1))
         def _():
             for each in copies():
                 each.wait()

time: 105 us -> 104 us (level)
  no operation moved by 1% of the time
where the time goes in v3:
time: 104 us
  starting transfers between devices  52.1 us (50%)
  waiting for transfers between devices  37.2 us (36%)
  Pallas kernels  12 us (12%)
  matrix products  1.55 us (1%)
    ppermute x1, starting transfers between devices, body(): near = lax.ppermute(low, 'ba', across)  18.2 us
    ppermute x1, waiting for transfers between devices, body(): far = lax.ppermute(sibling, 'ba', across)  12.2 us
    ppermute x1, waiting for transfers between devices, body(): near = lax.ppermute(low, 'ba', across)  8.97 us
    ppermute x1, starting transfers between devices, body(): lax.ppermute(pair, 'aa', [(i, i ^ 12) for i in range(rows)])  7.64 us
    ppermute x1, starting transfers between devices, body(): lax.ppermute(got, 'aa', [(i, i ^ 4) for i in range(rows)])  6.28 us
    ppermute x1, waiting for transfers between devices, body(): next_far = lax.ppermute(far, 'ba', within)  5.09 us
    ppermute x4, waiting for transfers between devices, body(): lax.ppermute(held[step], BOTH, spread_pairs(step, cols))  4.97 us
    pallas_call x1, Pallas kernels, prepare(): pl.pallas_call(kernel, grid=(steps,), out_shape=(jax.ShapeDtypeStruct(coe...  4.08 us
  transfers between devices with their start and end apart: 15, of which 6 were waited for; matrix products, arithmetic and copies ran while one was open for 0% of the time, Pallas kernels for 8%

profile of v3, /device:TPU:8, one launch (start us, length us, event | category | flops | bytes accessed | tf_op | source)
XLA Modules:
  0.0 103.5 jit_solution(13118684136709412077)
XLA Ops:
  0.0 4.1 %prepare.1 = (bf16[768,384]{1,0:T(8,128)(2,1)}, bf16[4,6,48,384]{3,2,1,0:T(8,128)(2,1)}, bf16[4,6,48,384]{3,2,1,0:T(8,128)(2,1)}) custom-call(s32[1,3]{1,0:T(1,128)} %cols_ref.3, bf16[1,3,768,768]{3,2,1,0:T(8,128)(2,1)} %tiles_ref.3, f32[768,384]{1,0:T(8,128)} %full_ref.3), custom_call_target="tpu_custom_call" | custom-call | tf_op jit(solution)/shard_map/prepare/pallas_call | solution.py:60
  4.1 0.7 collective-permute-start.2
  4.9 0.1 broadcast_select_fusion
  5.0 0.1 slice_bitcast_fusion
  5.1 1.4 %collective-permute-start.3 = (bf16[6,48,384]{2,1,0:T(8,128)(2,1)S(1)}, bf16[6,48,384]{2,1,0:T(8,128)(2,1)S(1)}, u32[]{:S(2)}, u32[]{:S(2)}) collective-permute-start(bf16[6,48,384]{2,1,0:T(8,128)(2,1)S(1)} %get-tuple-element.18), channel_id=1, source_target_pairs={{0,0},{16,64},{32,32},{48,96},{1,1},{17,65},{33,33},{49,97},{2,2},... | collective-permute-start | bytes 663560 | tf_op jit(solution)/shard_map/ppermute | solution.py:254
  6.5 0.7 collective-permute-start.4
  7.2 0.7 collective-permute-start.5
  7.9 0.7 collective-permute-start.6
  8.6 3.8 %collective-permute-start.10 = (bf16[768,384]{1,0:T(8,128)(2,1)S(1)}, bf16[768,384]{1,0:T(8,128)(2,1)S(1)}, u32[]{:S(2)}, u32[]{:S(2)}) collective-permute-start(bf16[768,384]{1,0:T(8,128)(2,1)S(1)} %copy-done.2), channel_id=1, source_target_pairs={{0,1},{1,0},{2,3},{3,2},{4,5},{5,4},{6,7},{7,6},{8,9},{9,8},{10,11... | collective-permute-start | bytes 1769480 | tf_op jit(solution)/shard_map/ppermute | solution.py:247
  12.4 5.0 %collective-permute-done.3.refs_0_ = bf16[6,48,384]{2,1,0:T(8,128)(2,1)S(1)} collective-permute-done((bf16[6,48,384]{2,1,0:T(8,128)(2,1)S(1)}, bf16[6,48,384]{2,1,0:T(8,128)(2,1)S(1)}, u32[]{:S(2)}, u32[]{:S(2)}) %collective-permute-start.3) | collective-permute-done | bytes 221216 | tf_op jit(solution)/shard_map/ppermute | solution.py:254
  17.4 0.3 choose.1.refs_0_
  17.8 0.0 copy-start.4
  17.8 6.3 %collective-permute-start.7 = (bf16[6,48,384]{2,1,0:T(8,128)(2,1)S(1)}, bf16[6,48,384]{2,1,0:T(8,128)(2,1)S(1)}, u32[]{:S(2)}, u32[]{:S(2)}) collective-permute-start(bf16[6,48,384]{2,1,0:T(8,128)(2,1)S(1)} %choose.1.refs_0_), channel_id=1, source_target_pairs={{0,128},{32,160},{64,192},{96,224},{128,0},{160,32},{192,64},{224,... | collective-permute-start | bytes 663560 | tf_op jit(solution)/shard_map/ppermute | solution.py:263
  24.1 3.9 %collective-permute-done.7.refs_1_ = bf16[6,48,384]{2,1,0:T(8,128)(2,1)S(1)} collective-permute-done((bf16[6,48,384]{2,1,0:T(8,128)(2,1)S(1)}, bf16[6,48,384]{2,1,0:T(8,128)(2,1)S(1)}, u32[]{:S(2)}, u32[]{:S(2)}) %collective-permute-start.7) | collective-permute-done | bytes 221216 | tf_op jit(solution)/shard_map/ppermute | solution.py:263
  28.0 0.6 stack.2.refs_0_
  28.5 7.6 %collective-permute-start.8 = (bf16[2,6,48,384]{3,2,1,0:T(8,128)(2,1)S(1)}, bf16[2,6,48,384]{3,2,1,0:T(8,128)(2,1)S(1)}, u32[]{:S(2)}, u32[]{:S(2)}) collective-permute-start(bf16[2,6,48,384]{3,2,1,0:T(8,128)(2,1)S(1)} %stack.2.refs_0_), channel_id=1, source_target_pairs={{0,384},{32,416},{64,448},{96,480},{128,256},{160,288},{192,320},{... | collective-permute-start | bytes 1327112 | tf_op jit(solution)/shard_map/ppermute | solution.py:264
  36.2 18.2 %collective-permute-start.12 = (bf16[768,384]{1,0:T(8,128)(2,1)S(1)}, bf16[768,384]{1,0:T(8,128)(2,1)S(1)}, u32[]{:S(2)}, u32[]{:S(2)}) collective-permute-start(bf16[768,384]{1,0:T(8,128)(2,1)S(1)} %copy-done.2), channel_id=1, source_target_pairs={{0,31},{1,2},{2,1},{3,4},{4,3},{5,6},{6,5},{7,8},{8,7},{9,10},{10,... | collective-permute-start | bytes 1769480 | tf_op jit(solution)/shard_map/ppermute | solution.py:246
  54.4 1.9 %collective-permute-start.11 = (bf16[768,384]{1,0:T(8,128)(2,1)S(1)}, bf16[768,384]{1,0:T(8,128)(2,1)S(1)}, u32[]{:S(2)}, u32[]{:S(2)}) collective-permute-start(bf16[768,384]{1,0:T(8,128)(2,1)S(1)} %collective-permute-done.10.refs_6_), channel_id=1, source_target_pairs={{0,31},{1,2},{2,1},{3,4},{4,3},{5,6},{6,5},{7,8},{8,7},{9,10},{10,... | collective-permute-start | bytes 1769480 | tf_op jit(solution)/shard_map/ppermute | solution.py:259
  56.3 0.5 stack.3.refs_1_
  56.8 1.9 %collective-permute-start.9 = (bf16[4,6,48,384]{3,2,1,0:T(8,128)(2,1)S(1)}, bf16[4,6,48,384]{3,2,1,0:T(8,128)(2,1)S(1)}, u32[]{:S(2)}, u32[]{:S(2)}) collective-permute-start(bf16[4,6,48,384]{3,2,1,0:T(8,128)(2,1)S(1)} %stack.3.refs_1_), channel_id=1, source_target_pairs={{0,32},{32,0},{64,96},{96,64},{128,160},{160,128},{192,224},{224,1... | collective-permute-start | bytes 2654216 | tf_op jit(solution)/shard_map/ppermute | solution.py:265
  58.8 1.9 %collective-permute-start = (bf16[768,384]{1,0:T(8,128)(2,1)S(1)}, bf16[768,384]{1,0:T(8,128)(2,1)S(1)}, u32[]{:S(2)}, u32[]{:S(2)}) collective-permute-start(bf16[768,384]{1,0:T(8,128)(2,1)S(1)} %copy-done.2), channel_id=1, source_target_pairs={{0,480},{32,64},{64,32},{96,128},{128,96},{160,192},{192,160},{224... | collective-permute-start | bytes 1769480 | tf_op jit(solution)/shard_map/ppermute | solution.py:257
  60.7 2.4 %collective-permute-start.1 = (bf16[768,384]{1,0:T(8,128)(2,1)S(1)}, bf16[768,384]{1,0:T(8,128)(2,1)S(1)}, u32[]{:S(2)}, u32[]{:S(2)}) collective-permute-start(bf16[768,384]{1,0:T(8,128)(2,1)S(1)} %copy-done.2), channel_id=1, source_target_pairs={{0,32},{32,0},{64,96},{96,64},{128,160},{160,128},{192,224},{224,1... | collective-permute-start | bytes 1769480 | tf_op jit(solution)/shard_map/ppermute | solution.py:258
  63.1 9.0 %collective-permute-done.12.refs_4_ = bf16[768,384]{1,0:T(8,128)(2,1)S(1)} collective-permute-done((bf16[768,384]{1,0:T(8,128)(2,1)S(1)}, bf16[768,384]{1,0:T(8,128)(2,1)S(1)}, u32[]{:S(2)}, u32[]{:S(2)}) %collective-permute-start.12) | collective-permute-done | bytes 589856 | tf_op jit(solution)/shard_map/ppermute | solution.py:246
  72.1 1.9 %collective-permute-start.13 = (bf16[768,384]{1,0:T(8,128)(2,1)S(1)}, bf16[768,384]{1,0:T(8,128)(2,1)S(1)}, u32[]{:S(2)}, u32[]{:S(2)}) collective-permute-start(bf16[768,384]{1,0:T(8,128)(2,1)S(1)} %collective-permute-done.12.refs_4_), channel_id=1, source_target_pairs={{0,1},{1,0},{2,3},{3,2},{4,5},{5,4},{6,7},{7,6},{8,9},{9,8},{10,11... | collective-permute-start | bytes 1769480 | tf_op jit(solution)/shard_map/ppermute | solution.py:260
  74.0 12.2 %collective-permute-done.11.refs_3_ = bf16[768,384]{1,0:T(8,128)(2,1)S(1)} collective-permute-done((bf16[768,384]{1,0:T(8,128)(2,1)S(1)}, bf16[768,384]{1,0:T(8,128)(2,1)S(1)}, u32[]{:S(2)}, u32[]{:S(2)}) %collective-permute-start.11) | collective-permute-done | bytes 589856 | tf_op jit(solution)/shard_map/ppermute | solution.py:259
  86.2 1.9 %collective-permute-start.14 = (bf16[768,384]{1,0:T(8,128)(2,1)S(1)}, bf16[768,384]{1,0:T(8,128)(2,1)S(1)}, u32[]{:S(2)}, u32[]{:S(2)}) collective-permute-start(bf16[768,384]{1,0:T(8,128)(2,1)S(1)} %collective-permute-done.11.refs_3_), channel_id=1, source_target_pairs={{0,1},{1,0},{2,3},{3,2},{4,5},{5,4},{6,7},{7,6},{8,9},{9,8},{10,11... | collective-permute-start | bytes 1769480 | tf_op jit(solution)/shard_map/ppermute | solution.py:261
  88.1 0.2 broadcast_in_dim.8.alpha_ref
  88.3 2.1 %collective-permute-done.outer_ref = bf16[768,384]{1,0:T(8,128)(2,1)S(1)} collective-permute-done((bf16[768,384]{1,0:T(8,128)(2,1)S(1)}, bf16[768,384]{1,0:T(8,128)(2,1)S(1)}, u32[]{:S(2)}, u32[]{:S(2)}) %collective-permute-start) | collective-permute-done | bytes 589856 | tf_op jit(solution)/shard_map/ppermute | solution.py:257
  90.4 3.5 %alpha_part.1.refs_0_ = f32[768,384]{1,0:T(8,128)S(1)} custom-call(s32[1,3]{1,0:T(1,128)S(1)} %copy-done.3, bf16[1,3,768,768]{3,2,1,0:T(8,128)(2,1)S(1)} %copy-done, bf16[768,384]{1,0:T(8,128)(2,1)S(1)} %copy-done.2, bf16[768,384]{1,0:T(8,128)(2,1)S(1)} %collective-permute-done.outer_ref, bf16[768,384]{1,0:T(8,128)(2,1)S(1)} %collective-permute-done.1.swap_ref, ...), custom_call_target="tpu_custom_call" | custom-call | tf_op jit(solution)/shard_map/alpha_part/pallas_call | solution.py:151
  93.9 3.0 %beta_part.1 = (f32[768,384]{1,0:T(8,128)S(1)}, bf16[384,384]{1,0:T(8,128)(2,1)S(1)}) custom-call(f32[768,384]{1,0:T(8,128)S(1)} %alpha_part.1.refs_0_, bf16[4,6,48,384]{3,2,1,0:T(8,128)(2,1)S(1)} %stack.3.refs_1_, bf16[4,6,48,384]{3,2,1,0:T(8,128)(2,1)S(1)} %collective-permute-done.9.refs_2_, bf16[768,384]{1,0:T(8,128)(2,1)S(1)} %collective-permute-done.11.refs_3_, ...), custom_call_target="tpu_custom_call" | custom-call | tf_op jit(solution)/shard_map/beta_part/pallas_call | solution.py:201
  96.9 5.1 %collective-permute-done.14 = bf16[768,384]{1,0:T(8,128)(2,1)S(1)} collective-permute-done((bf16[768,384]{1,0:T(8,128)(2,1)S(1)}, bf16[768,384]{1,0:T(8,128)(2,1)S(1)}, u32[]{:S(2)}, u32[]{:S(2)}) %collective-permute-start.14) | collective-permute-done | bytes 589856 | tf_op jit(solution)/shard_map/ppermute | solution.py:261
  102.0 1.5 %convolution_add_fusion = f32[768,384]{1,0:T(8,128)} fusion(f32[768,384]{1,0:T(8,128)S(1)} %get-tuple-element.13, bf16[768,384]{1,0:T(8,128)(2,1)S(1)} %collective-permute-done.14, bf16[384,384]{1,0:T(8,128)(2,1)S(1)} %get-tuple-element.14), kind=kOutput, calls=%fused_computation | convolution fusion | flops 226787328 | bytes 3244032 | tf_op jit(solution)/shard_map/dot_general | solution.py:222
  (21 shorter events, 0.1 us)
Async XLA Ops:
  4.1 0.8 collective-permute-start.2
  5.0 3.6 %copy-start.2 = (bf16[768,384]{1,0:T(8,128)(2,1)S(1)}, bf16[768,384]{1,0:T(8,128)(2,1)}, u32[]{:S(2)}) copy-start(bf16[768,384]{1,0:T(8,128)(2,1)} %get-tuple-element.10.low_ref.refs_5_) | copy-start | bytes 1769476
  5.0 85.4 %copy-start.1 = (f32[768,384]{1,0:T(8,128)S(1)}, f32[768,384]{1,0:T(8,128)}, u32[]{:S(2)}) copy-start(f32[768,384]{1,0:T(8,128)} %full_ref.3) | copy-start | bytes 3538948
  5.1 12.3 %collective-permute-start.3 = (bf16[6,48,384]{2,1,0:T(8,128)(2,1)S(1)}, bf16[6,48,384]{2,1,0:T(8,128)(2,1)S(1)}, u32[]{:S(2)}, u32[]{:S(2)}) collective-permute-start(bf16[6,48,384]{2,1,0:T(8,128)(2,1)S(1)} %get-tuple-element.18), channel_id=1, source_target_pairs={{0,0},{16,64},{32,32},{48,96},{1,1},{17,65},{33,33},{49,97},{2,2},... | collective-permute-start | bytes 663560 | tf_op jit(solution)/shard_map/ppermute | solution.py:254
  6.5 10.9 %collective-permute-start.4 = (bf16[6,48,384]{2,1,0:T(8,128)(2,1)S(1)}, bf16[6,48,384]{2,1,0:T(8,128)(2,1)S(1)}, u32[]{:S(2)}, u32[]{:S(2)}) collective-permute-start(bf16[6,48,384]{2,1,0:T(8,128)(2,1)S(1)} %get-tuple-element.17), channel_id=1, source_target_pairs={{0,128},{16,192},{32,160},{48,224},{1,129},{17,193},{33,161},{49,2... | collective-permute-start | bytes 663560 | tf_op jit(solution)/shard_map/ppermute | solution.py:254
  7.2 10.2 %collective-permute-start.5 = (bf16[6,48,384]{2,1,0:T(8,128)(2,1)S(1)}, bf16[6,48,384]{2,1,0:T(8,128)(2,1)S(1)}, u32[]{:S(2)}, u32[]{:S(2)}) collective-permute-start(bf16[6,48,384]{2,1,0:T(8,128)(2,1)S(1)} %get-tuple-element.16), channel_id=1, source_target_pairs={{0,256},{16,320},{32,288},{48,352},{1,257},{17,321},{33,289},{49,3... | collective-permute-start | bytes 663560 | tf_op jit(solution)/shard_map/ppermute | solution.py:254
  7.9 9.5 %collective-permute-start.6 = (bf16[6,48,384]{2,1,0:T(8,128)(2,1)S(1)}, bf16[6,48,384]{2,1,0:T(8,128)(2,1)S(1)}, u32[]{:S(2)}, u32[]{:S(2)}) collective-permute-start(bf16[6,48,384]{2,1,0:T(8,128)(2,1)S(1)} %get-tuple-element.15), channel_id=1, source_target_pairs={{0,384},{16,448},{32,416},{48,480},{1,385},{17,449},{33,417},{49,4... | collective-permute-start | bytes 663560 | tf_op jit(solution)/shard_map/ppermute | solution.py:254
  8.6 45.8 %collective-permute-start.10 = (bf16[768,384]{1,0:T(8,128)(2,1)S(1)}, bf16[768,384]{1,0:T(8,128)(2,1)S(1)}, u32[]{:S(2)}, u32[]{:S(2)}) collective-permute-start(bf16[768,384]{1,0:T(8,128)(2,1)S(1)} %copy-done.2), channel_id=1, source_target_pairs={{0,1},{1,0},{2,3},{3,2},{4,5},{5,4},{6,7},{7,6},{8,9},{9,8},{10,11... | collective-permute-start | bytes 1769480 | tf_op jit(solution)/shard_map/ppermute | solution.py:247
  17.4 73.0 %copy-start = (bf16[1,3,768,768]{3,2,1,0:T(8,128)(2,1)S(1)}, bf16[1,3,768,768]{3,2,1,0:T(8,128)(2,1)}, u32[]{:S(2)}) copy-start(bf16[1,3,768,768]{3,2,1,0:T(8,128)(2,1)} %tiles_ref.3) | copy-start | bytes 10616836
  17.8 70.3 %copy-start.4 = (f32[768]{0:T(1024)S(1)}, f32[768]{0:T(1024)}, u32[]{:S(2)}) copy-start(f32[768]{0:T(1024)} %param.8) | copy-start | bytes 9220
  17.8 10.2 %collective-permute-start.7 = (bf16[6,48,384]{2,1,0:T(8,128)(2,1)S(1)}, bf16[6,48,384]{2,1,0:T(8,128)(2,1)S(1)}, u32[]{:S(2)}, u32[]{:S(2)}) collective-permute-start(bf16[6,48,384]{2,1,0:T(8,128)(2,1)S(1)} %choose.1.refs_0_), channel_id=1, source_target_pairs={{0,128},{32,160},{64,192},{96,224},{128,0},{160,32},{192,64},{224,... | collective-permute-start | bytes 663560 | tf_op jit(solution)/shard_map/ppermute | solution.py:263
  28.5 59.8 %copy-start.5 = (f32[384]{0:T(512)S(1)}, f32[384]{0:T(512)}, u32[]{:S(2)}) copy-start(f32[384]{0:T(512)} %param.9) | copy-start | bytes 4612
  28.5 61.8 %copy-start.3 = (s32[1,3]{1,0:T(1,128)S(1)}, s32[1,3]{1,0:T(1,128)}, u32[]{:S(2)}) copy-start(s32[1,3]{1,0:T(1,128)} %cols_ref.3) | copy-start | bytes 40
  28.5 27.8 %collective-permute-start.8 = (bf16[2,6,48,384]{3,2,1,0:T(8,128)(2,1)S(1)}, bf16[2,6,48,384]{3,2,1,0:T(8,128)(2,1)S(1)}, u32[]{:S(2)}, u32[]{:S(2)}) collective-permute-start(bf16[2,6,48,384]{3,2,1,0:T(8,128)(2,1)S(1)} %stack.2.refs_0_), channel_id=1, source_target_pairs={{0,384},{32,416},{64,448},{96,480},{128,256},{160,288},{192,320},{... | collective-permute-start | bytes 1327112 | tf_op jit(solution)/shard_map/ppermute | solution.py:264
  36.2 35.9 %collective-permute-start.12 = (bf16[768,384]{1,0:T(8,128)(2,1)S(1)}, bf16[768,384]{1,0:T(8,128)(2,1)S(1)}, u32[]{:S(2)}, u32[]{:S(2)}) collective-permute-start(bf16[768,384]{1,0:T(8,128)(2,1)S(1)} %copy-done.2), channel_id=1, source_target_pairs={{0,31},{1,2},{2,1},{3,4},{4,3},{5,6},{6,5},{7,8},{8,7},{9,10},{10,... | collective-permute-start | bytes 1769480 | tf_op jit(solution)/shard_map/ppermute | solution.py:246
  54.4 31.8 %collective-permute-start.11 = (bf16[768,384]{1,0:T(8,128)(2,1)S(1)}, bf16[768,384]{1,0:T(8,128)(2,1)S(1)}, u32[]{:S(2)}, u32[]{:S(2)}) collective-permute-start(bf16[768,384]{1,0:T(8,128)(2,1)S(1)} %collective-permute-done.10.refs_6_), channel_id=1, source_target_pairs={{0,31},{1,2},{2,1},{3,4},{4,3},{5,6},{6,5},{7,8},{8,7},{9,10},{10,... | collective-permute-start | bytes 1769480 | tf_op jit(solution)/shard_map/ppermute | solution.py:259
  56.8 37.0 %collective-permute-start.9 = (bf16[4,6,48,384]{3,2,1,0:T(8,128)(2,1)S(1)}, bf16[4,6,48,384]{3,2,1,0:T(8,128)(2,1)S(1)}, u32[]{:S(2)}, u32[]{:S(2)}) collective-permute-start(bf16[4,6,48,384]{3,2,1,0:T(8,128)(2,1)S(1)} %stack.3.refs_1_), channel_id=1, source_target_pairs={{0,32},{32,0},{64,96},{96,64},{128,160},{160,128},{192,224},{224,1... | collective-permute-start | bytes 2654216 | tf_op jit(solution)/shard_map/ppermute | solution.py:265
  58.8 31.6 %collective-permute-start = (bf16[768,384]{1,0:T(8,128)(2,1)S(1)}, bf16[768,384]{1,0:T(8,128)(2,1)S(1)}, u32[]{:S(2)}, u32[]{:S(2)}) collective-permute-start(bf16[768,384]{1,0:T(8,128)(2,1)S(1)} %copy-done.2), channel_id=1, source_target_pairs={{0,480},{32,64},{64,32},{96,128},{128,96},{160,192},{192,160},{224... | collective-permute-start | bytes 1769480 | tf_op jit(solution)/shard_map/ppermute | solution.py:257
  60.7 29.7 %collective-permute-start.1 = (bf16[768,384]{1,0:T(8,128)(2,1)S(1)}, bf16[768,384]{1,0:T(8,128)(2,1)S(1)}, u32[]{:S(2)}, u32[]{:S(2)}) collective-permute-start(bf16[768,384]{1,0:T(8,128)(2,1)S(1)} %copy-done.2), channel_id=1, source_target_pairs={{0,32},{32,0},{64,96},{96,64},{128,160},{160,128},{192,224},{224,1... | collective-permute-start | bytes 1769480 | tf_op jit(solution)/shard_map/ppermute | solution.py:258
  72.1 21.8 %collective-permute-start.13 = (bf16[768,384]{1,0:T(8,128)(2,1)S(1)}, bf16[768,384]{1,0:T(8,128)(2,1)S(1)}, u32[]{:S(2)}, u32[]{:S(2)}) collective-permute-start(bf16[768,384]{1,0:T(8,128)(2,1)S(1)} %collective-permute-done.12.refs_4_), channel_id=1, source_target_pairs={{0,1},{1,0},{2,3},{3,2},{4,5},{5,4},{6,7},{7,6},{8,9},{9,8},{10,11... | collective-permute-start | bytes 1769480 | tf_op jit(solution)/shard_map/ppermute | solution.py:260
  86.2 15.8 %collective-permute-start.14 = (bf16[768,384]{1,0:T(8,128)(2,1)S(1)}, bf16[768,384]{1,0:T(8,128)(2,1)S(1)}, u32[]{:S(2)}, u32[]{:S(2)}) collective-permute-start(bf16[768,384]{1,0:T(8,128)(2,1)S(1)} %collective-permute-done.11.refs_3_), channel_id=1, source_target_pairs={{0,1},{1,0},{2,3},{3,2},{4,5},{5,4},{6,7},{7,6},{8,9},{9,8},{10,11... | collective-permute-start | bytes 1769480 | tf_op jit(solution)/shard_map/ppermute | solution.py:261
